TPU v7x, 32 devices: a whole 2x2x4 slice. The times are simulated.
32 devices in a mesh: group: 4 (over y, x), member: 8 (over z, core).
Axes of the slice: x: 2, y: 2, z: 4, core: 2. Of those that a mesh axis runs over, the one named last changes fastest.
Arguments:
- tokens: bfloat16 [4096, 1024], P(('group', 'member')), may hold values from -420 to 420
- latents: bfloat16 [1024, 1024], P('member'), may hold values from -420 to 420
- tok_gain: float32 [1024], replicated, may hold values from 0.5 to 1.5
- lat_gain: float32 [1024], replicated, may hold values from 0.5 to 1.5
- mlp_gain: float32 [1024], replicated, may hold values from 0.5 to 1.5
- w_ref_tok: bfloat16 [1024, 1024], replicated, may hold values from -1.15625 to 1.15625
- w_val_tok: bfloat16 [1024, 1024], replicated, may hold values from -0.75 to 0.75
- w_out_tok: bfloat16 [1024, 1024], replicated, may hold values from -0.1875 to 0.1875
- w_ref_lat: bfloat16 [1024, 1024], P('member'), may hold values from -1.15625 to 1.15625
- w_val_lat: bfloat16 [1024, 1024], P('member'), may hold values from -0.75 to 0.75
- w_out_lat: bfloat16 [1024, 1024], P('member'), may hold values from -0.1875 to 0.1875
- w_up: bfloat16 [1024, 2048], P(None, 'member'), may hold values from -0.1875 to 0.1875
- w_down: bfloat16 [2048, 1024], P('member'), may hold values from -0.125 to 0.125
Outputs:
- tokens_out: bfloat16 [4096, 1024], P(('group', 'member'))
- latents_out: bfloat16 [1024, 1024], P('member')
All inputs are finite; a program needn't handle non-finite values.
Results may differ from a plain program's by a relative error of at most 0.005.
The roundings to bfloat16 on the way count: a program that leaves them out, or rounds other values in their place, can miss the bound.
Values may be sent and summed in bfloat16 or wider, within the bound.
No kernel may reach another device: no remote copies, remote signals or barrier semaphores. Data moves between devices by JAX's collectives and lax.ppermute only.
A program may use at most 128 MiB of HBM per device.

v0:
```python
import functools

import jax
import jax.numpy as jnp
from jax import lax
from jax.experimental import pallas as pl
from jax.experimental.pallas import tpu as pltpu
from jax.sharding import PartitionSpec as P


HEAD_DIM = 64
NORM_EPS = 1e-06
LOG2E = 1.4426950408889634
RATE = HEAD_DIM ** (-0.5) * LOG2E
LANES = 128
MLP_PEERS = 4
BF16 = jnp.bfloat16
F32 = jnp.float32


VMEM = pl.BlockSpec(memory_space=pltpu.VMEM)
SMEM = pl.BlockSpec(memory_space=pltpu.SMEM)


def normalize(values):
    return values * lax.rsqrt(jnp.mean(values * values, axis=-1, keepdims=True) + NORM_EPS)


def project(left_side, right_side):
    return jnp.dot(left_side, right_side, preferred_element_type=F32)


def project_t(left_side, right_side):
    return lax.dot_general(
        left_side, right_side, (((1,), (1,)), ((), ())), preferred_element_type=F32
    )


def swap(x, axis, offset):
    size = lax.axis_size(axis)
    return lax.ppermute(x, axis, [(i, i ^ offset) for i in range(size)])


def gathered(x, axis, step):
    size = lax.axis_size(axis)
    return [x] + [swap(x, axis, k) for k in range(step, size, step)]


def call(body, outs, ins, flops, scratch=()):
    moved = sum(x.size * x.dtype.itemsize for x in ins) + sum(
        o.size * o.dtype.itemsize for o in outs
    )
    return pl.pallas_call(
        body,
        out_shape=outs,
        in_specs=[SMEM if x.dtype == jnp.int32 else VMEM for x in ins],
        out_specs=[VMEM] * len(outs),
        scratch_shapes=list(scratch),
        compiler_params=pltpu.CompilerParams(vmem_limit_bytes=48 * 1024 * 1024),
        cost_estimate=pl.CostEstimate(flops=flops, bytes_accessed=moved, transcendentals=0),
    )(*ins)


def aligned(index, multiple):
    return pl.multiple_of(index * multiple, multiple)


def shape(dims, dtype):
    return jax.ShapeDtypeStruct(dims, dtype)


def head_lanes(width):
    return lax.broadcasted_iota(jnp.int32, (1, width), 1) // HEAD_DIM


def only(values, lanes, head):
    return jnp.where(lanes == head, values, jnp.zeros_like(values))


def side_by_side(pair, width):
    pad = ((0, 0), (0, -width % LANES))
    return jnp.concatenate([jnp.pad(w, pad) for w in pair], 1)


def from_group(x, where, size, dim):
    return lax.dynamic_slice_in_dim(x, where[0] * size, size, dim)


def queries(tok_near, gain, w_ref, w_val, where, width):
    near = len(tok_near)
    n_own, features = tok_near[0].shape
    if width % LANES:
        normed = (normalize(jnp.concatenate(tok_near, 0).astype(F32)) * gain).astype(BF16)
        return side_by_side(
            [project(normed, from_group(w, where, width, 1)).astype(BF16) for w in (w_ref, w_val)],
            width,
        )

    def body(*refs):
        toks, gain_ref, ref_w, val_w = refs[1 : 1 + near], *refs[1 + near : 4 + near]
        out, normed = refs[4 + near :]
        for k in range(near):
            rows = slice(k * n_own, (k + 1) * n_own)
            normed[rows, :] = (normalize(toks[k][...].astype(F32)) * gain_ref[...]).astype(BF16)
        out[:, :width] = project(normed[...], ref_w[...]).astype(BF16)
        out[:, width:] = project(normed[...], val_w[...]).astype(BF16)

    col_spec = pl.BlockSpec((features, width), lambda i, pos: (0, pos[0]))
    return pl.pallas_call(
        body,
        out_shape=shape((near * n_own, 2 * width), BF16),
        grid_spec=pltpu.PrefetchScalarGridSpec(
            num_scalar_prefetch=1,
            grid=(1,),
            in_specs=[
                *[pl.BlockSpec((n_own, features), lambda i, pos: (0, 0))] * near,
                pl.BlockSpec((1, features), lambda i, pos: (0, 0)),
                col_spec,
                col_spec,
            ],
            out_specs=pl.BlockSpec((near * n_own, 2 * width), lambda i, pos: (0, 0)),
            scratch_shapes=[pltpu.VMEM((near * n_own, features), BF16)],
        ),
        cost_estimate=pl.CostEstimate(
            flops=4 * near * n_own * features * width,
            bytes_accessed=2 * (near * n_own + 2 * width) * features,
            transcendentals=0,
        ),
        name="queries",
    )(where, *tok_near, gain.reshape(1, -1), w_ref, w_val)


def prepare(latents, gain, w_ref, w_val, w_out, w_up, w_down, where):
    n_group = lax.axis_size("group")
    rows, features = latents.shape
    share, width = rows // n_group, features // n_group
    ff = w_up.shape[1] // n_group
    w_rows = w_ref.shape[0]
    slab = w_rows // n_group
    if width % LANES or share % 16 or slab % 16 or ff % 16 or LANES % ff:
        lat = normalize(from_group(latents, where, share, 0).astype(F32)) * gain
        out_cols = from_group(w_out, where, width, 1)
        return (
            lat.astype(BF16),
            side_by_side([from_group(w, where, width, 1) for w in (w_ref, w_val)], width),
            jnp.concatenate(
                [
                    jnp.transpose(from_group(w_up, where, ff, 1)),
                    from_group(w_down, where, ff, 0),
                    jnp.concatenate(
                        [out_cols[i * slab : (i + 1) * slab] for i in range(n_group)], 1
                    ),
                ],
                0,
            ),
        )

    def body(pos, lat_ref, gain_ref, ref_w, val_w, out_w, up_w, down_w, lat, cols, rest, turned):
        lat[...] = (normalize(lat_ref[...].astype(F32)) * gain_ref[...]).astype(BF16)
        cols[:, :width] = ref_w[...]
        cols[:, width:] = val_w[...]
        turned[...] = jnp.transpose(up_w[...].astype(F32))
        first = aligned(lax.rem(pos[0], LANES // ff), ff)
        rest[:ff, :] = turned[pl.ds(first, ff), :].astype(BF16)
        rest[ff : 2 * ff, :] = down_w[...]
        for i in range(n_group):
            rest[2 * ff :, i * width : (i + 1) * width] = out_w[i * slab : (i + 1) * slab, :]

    col_spec = pl.BlockSpec((w_rows, width), lambda i, pos: (0, pos[0]))
    outs = ((share, features), (w_rows, 2 * width), (2 * ff + slab, features))
    return pl.pallas_call(
        body,
        out_shape=[shape(o, BF16) for o in outs],
        grid_spec=pltpu.PrefetchScalarGridSpec(
            num_scalar_prefetch=1,
            grid=(1,),
            in_specs=[
                pl.BlockSpec((share, features), lambda i, pos: (pos[0], 0)),
                pl.BlockSpec((1, features), lambda i, pos: (0, 0)),
                col_spec,
                col_spec,
                col_spec,
                pl.BlockSpec((features, LANES), lambda i, pos: (0, pos[0] // (LANES // ff))),
                pl.BlockSpec((ff, features), lambda i, pos: (pos[0], 0)),
            ],
            out_specs=[pl.BlockSpec(o, lambda i, pos: (0, 0)) for o in outs],
            scratch_shapes=[pltpu.VMEM((LANES, features), F32)],
        ),
        cost_estimate=pl.CostEstimate(flops=0, bytes_accessed=4 * 1024 * 1024, transcendentals=0),
        name="prepare",
    )(where, latents, gain.reshape(1, -1), w_ref, w_val, w_out, w_up, w_down)


def stack_rows(parts):
    rows, cols = parts[0].shape

    def body(*refs):
        for k, part in enumerate(refs[:-1]):
            refs[-1][k * rows : (k + 1) * rows, :] = part[...]

    return call(body, [shape((len(parts) * rows, cols), parts[0].dtype)], parts, 0)[0]


def keys(lat_near, w_own, w_far, where):
    near, n_z = len(lat_near), len(w_own)
    rows, features = lat_near[0].shape
    w_rows, cols = w_own[0].shape

    def body(*refs):
        pos, lats = refs[0], refs[1 : 1 + near]
        own, far = refs[1 + near : 1 + near + n_z], refs[1 + near + n_z : 1 + near + 2 * n_z]
        out, w_all, lat_all = refs[-3:]
        for core, pieces in enumerate((own, far)):
            for j, piece in enumerate(pieces):
                w_all[pl.ds(aligned(pos[1] ^ (2 * j + core), w_rows), w_rows), :] = piece[...]
        for k in range(near):
            lat_all[k * rows : (k + 1) * rows, :] = lats[k][...]
        out[...] = project(lat_all[...], w_all[...]).astype(BF16)

    return call(
        body,
        [shape((near * rows, cols), BF16)],
        [where, *lat_near, *w_own, *w_far],
        2 * near * rows * features * cols,
        [pltpu.VMEM((features, cols), BF16), pltpu.VMEM((near * rows, features), BF16)],
    )[0]


def columns(qv_own, qv_far, kv_own, near, n_z, share, width):
    n_tok, pad = qv_own.shape[0], qv_own.shape[1] // 2
    heads = width // HEAD_DIM
    block = n_z * share
    group = 2 if near % 2 == 0 else 1
    step = group * block

    def body(own, far, k_ref, *outs):
        lanes = head_lanes(width)
        stat_lanes = lax.broadcasted_iota(jnp.int32, (1, LANES), 1)
        for first in range(0, near, group):
            k_rows = k_ref[first * block : first * block + step, :width]
            mixed = jnp.zeros((step, width), F32)
            scale = jnp.zeros((step, width), F32)
            stats = jnp.zeros((step, LANES), F32)
            for head in range(heads):
                k_head = only(k_rows, lanes, head)
                scores = [project_t(k_head, qv[:, :width]) for qv in (own, far)]
                peak = jnp.maximum(*[jnp.max(s, axis=1, keepdims=True) for s in scores])
                powers = [jnp.exp2((s - peak) * RATE) for s in scores]
                total = sum(jnp.sum(e, axis=1, keepdims=True) for e in powers)
                for e, qv in zip(powers, (own, far)):
                    mixed += project(e.astype(BF16), only(qv[:, pad : pad + width], lanes, head))
                scale = jnp.where(lanes == head, 1.0 / total, scale)
                stats = jnp.where(stat_lanes == head, peak * RATE + jnp.log2(total), stats)
            mixed = (mixed * scale).astype(BF16)
            high = stats.astype(BF16).astype(F32)
            middle = (stats - high).astype(BF16).astype(F32)
            low = stats - high - middle
            packed = high + pltpu.roll(middle, 32, 1) + pltpu.roll(low, 64, 1)
            packed = packed.astype(BF16)
            for k in range(group):
                for j in range(n_z):
                    rows = slice(k * block + j * share, k * block + (j + 1) * share)
                    to = slice((first + k) * share, (first + k + 1) * share)
                    outs[j][to, :width] = mixed[rows]
                    if width < pad:
                        outs[j][to, width:pad] = jnp.zeros((share, pad - width), BF16)
                    outs[j][to, pad:] = packed[rows]

    outs = [shape((near * share, pad + LANES), BF16)] * n_z
    flops = 16 * near * block * n_tok * width
    return call(body, outs, [qv_own, qv_far, kv_own], flops)


def rows_part(qv, kv_own, kv_far, width, n_own, peers):
    n_tok = qv.shape[0]
    half, pad2 = kv_own.shape
    pad = pad2 // 2
    heads = width // HEAD_DIM
    near = n_tok // n_own

    def body(q_ref, own, far, *outs):
        lanes = head_lanes(width)
        group = 2 if near % 2 == 0 else 1
        for first in range(0, near, group):
            q_rows = q_ref[first * n_own : (first + group) * n_own, :width]
            mixed = jnp.zeros((group * n_own, width), F32)
            for head in range(heads):
                q_head = only(q_rows, lanes, head)
                s_own = project_t(q_head, own[:, :width])
                s_far = project_t(q_head, far[:, :width])
                peak = jnp.maximum(
                    jnp.max(s_own, axis=1, keepdims=True), jnp.max(s_far, axis=1, keepdims=True)
                )
                e_own = jnp.exp2((s_own - peak) * RATE)
                e_far = jnp.exp2((s_far - peak) * RATE)
                inverse = 1.0 / (
                    jnp.sum(e_own, axis=1, keepdims=True) + jnp.sum(e_far, axis=1, keepdims=True)
                )
                mixed += project(
                    (e_own * inverse).astype(BF16), only(own[:, pad : pad + width], lanes, head)
                )
                mixed += project(
                    (e_far * inverse).astype(BF16), only(far[:, pad : pad + width], lanes, head)
                )
            mixed = mixed.astype(BF16)
            for b in range(group):
                for k in range(near):
                    t = (first + b) ^ k
                    if t < peers:
                        outs[k][t * n_own : (t + 1) * n_own, :] = mixed[
                            b * n_own : (b + 1) * n_own
                        ]

    outs = [shape((peers * n_own, width), BF16)] * near
    return call(body, outs, [qv, kv_own, kv_far], 8 * half * n_tok * width * 2)


def spread(stats, heads):
    rows = stats.shape[0]
    return jnp.concatenate(
        [jnp.broadcast_to(stats[:, h : h + 1], (rows, HEAD_DIM)) for h in range(heads)], 1
    )


def weighted(parts, stats, heads):
    peak = functools.reduce(jnp.maximum, stats)
    weights = [jnp.exp2(s - peak) for s in stats]
    total = sum(weights)
    mixed = sum(a * spread(w / total, heads) for a, w in zip(parts, weights))
    return mixed, peak + jnp.log2(total)


def join_members(parts, where, near, share, width):
    lat_own = parts[0].shape[0]
    pad = parts[0].shape[1] - LANES
    heads = width // HEAD_DIM

    def body(*refs):
        pos, ins, out = refs[0], refs[1:-1], refs[-1]
        for k in range(near):
            rows = slice(k * share, (k + 1) * share)
            packed = [p[rows, pad:].astype(F32) for p in ins]
            stats = [s + pltpu.roll(s, LANES - 32, 1) + pltpu.roll(s, LANES - 64, 1) for s in packed]
            mixed, _ = weighted([p[rows, :width].astype(F32) for p in ins], stats, heads)
            out[pl.ds(aligned(pos[0] ^ k, share), share), :] = mixed

    return call(body, [shape((lat_own, width), F32)], [where, *parts], 0)[0]


def latents_part(near_avg, lat_cols, own, far, where, n_share):
    near, n_z = len(near_avg), len(own)
    lat_own, width = near_avg[0].shape
    slab = own[0].shape[0] - 2 * n_share
    features = near * width

    def body(*refs):
        pos, avgs, lat = refs[0], refs[1 : 1 + near], refs[1 + near]
        own_w, far_w = refs[2 + near : 2 + near + n_z], refs[2 + near + n_z : 2 + near + 2 * n_z]
        out, w_all = refs[-2:]
        w_rows = near * slab
        for core, pieces in enumerate((own_w, far_w)):
            for j, piece in enumerate(pieces):
                for i in range(near):
                    to = aligned(pos[1] ^ (2 * j + core), w_rows) + i * slab
                    w_all[pl.ds(to, slab), :] = piece[
                        2 * n_share :, i * width : (i + 1) * width
                    ].astype(F32)
        values = [a[...] for a in avgs]
        square = sum(jnp.sum(a * a, axis=1, keepdims=True) for a in values)
        rate = lax.rsqrt(square * (1.0 / features) + NORM_EPS)
        total = lat[...].astype(F32)
        for k in range(near):
            total += project(
                (values[k] * rate).astype(BF16),
                w_all[pl.ds(aligned(pos[0] ^ k, width), width), :].astype(BF16),
            )
        out[...] = total.astype(BF16)

    return call(
        body,
        [shape((lat_own, width), BF16)],
        [where, *near_avg, lat_cols, *own, *far],
        2 * lat_own * features * width,
        [pltpu.VMEM((features, width), F32)],
    )[0]


def token_mlp(parts, tok_near, w_out, gain, own, far, where, n_share):
    near, peers, n_ff = len(parts), len(tok_near), len(own) + len(far)
    width = parts[0].shape[1]
    n_own, features = tok_near[0].shape

    def body(*refs):
        pos, w_ref, gain_ref = refs[:3]
        ins = refs[3 : 3 + near]
        toks = refs[3 + near : 3 + near + peers]
        ff = refs[3 + near + peers : 3 + near + peers + n_ff]
        own_out, sends = refs[3 + near + peers + n_ff], refs[4 + near + peers + n_ff : -2]
        up_t, down = refs[-2:]
        for i, piece in enumerate(ff):
            rows = slice(i * n_share, (i + 1) * n_share)
            up_t[rows, :] = piece[:n_share, :]
            down[rows, :] = piece[n_share : 2 * n_share, :]
        group = 2 if peers % 2 == 0 else 1
        for t in range(0, peers, group):
            rows = slice(t * n_own, (t + group) * n_own)
            mid = jnp.concatenate([toks[t + b][...].astype(F32) for b in range(group)], 0)
            for k in range(near):
                mid += project(
                    ins[k][rows, :], w_ref[pl.ds(aligned(pos[0] ^ k, width), width), :]
                )
            mlp_in = (normalize(mid) * gain_ref[...]).astype(BF16)
            hidden = project_t(mlp_in, up_t[...])
            hidden = (hidden * (0.5 + 0.5 * lax.erf(hidden * (0.5**0.5)))).astype(BF16)
            partial = project(hidden, down[...])
            for b in range(group):
                rows = slice(b * n_own, (b + 1) * n_own)
                if t + b == 0:
                    own_out[...] = mid[rows] + partial[rows]
                else:
                    sends[t + b - 1][...] = partial[rows].astype(BF16)

    ff_rows = n_ff * n_share
    return call(
        body,
        [shape((n_own, features), F32)] + [shape((n_own, features), BF16)] * (peers - 1),
        [where, w_out, gain.reshape(1, -1), *parts, *tok_near, *own, *far],
        2 * peers * n_own * features * (features + 2 * ff_rows),
        [pltpu.VMEM((ff_rows, features), BF16)] * 2,
    )


def finish(own, received, lat_parts, where):
    rows, width = lat_parts[0].shape
    n_in = 1 + len(received)
    near = len(lat_parts)
    lat_shape = shape((rows, near * width), BF16)
    if width % LANES:
        order = jnp.arange(near) ^ where[0]
        placed = jnp.transpose(jnp.take(jnp.stack(lat_parts), order, axis=0), (1, 0, 2))
        total = own + sum(r.astype(F32) for r in received)
        return total.astype(BF16), placed.reshape(lat_shape.shape)

    def body(*refs):
        pos, ins, parts = refs[0], refs[1 : 1 + n_in], refs[1 + n_in : -2]
        for k, part in enumerate(parts):
            refs[-1][:, pl.ds(aligned(pos[0] ^ k, width), width)] = part[...]
        refs[-2][...] = sum(r[...].astype(F32) for r in ins).astype(BF16)

    outs = [shape(own.shape, BF16), lat_shape]
    return call(body, outs, [where, own, *received, *lat_parts], 0)


def per_device(
    tokens,
    latents,
    tok_gain,
    lat_gain,
    mlp_gain,
    w_ref_tok,
    w_val_tok,
    w_out_tok,
    w_ref_lat,
    w_val_lat,
    w_out_lat,
    w_up,
    w_down,
):
    n_group, n_member = lax.axis_size("group"), lax.axis_size("member")
    n_z = n_member // 2
    g, m = lax.axis_index("group"), lax.axis_index("member")
    where = jnp.stack([g, m]).astype(jnp.int32)
    n_own, features = tokens.shape
    lat_own = latents.shape[0]
    width, share = features // n_group, lat_own // n_group
    ff_share = w_up.shape[1] // n_group
    peers = min(n_group, MLP_PEERS)

    tok_near = gathered(tokens, "group", 1)
    lat_part, w_mine, ff_mine = prepare(
        latents, lat_gain, w_ref_lat, w_val_lat, w_out_lat, w_up, w_down, where
    )
    lat_col = gathered(lat_part, "member", 2)
    w_own = gathered(w_mine, "member", 2)
    lat_near = gathered(stack_rows(lat_col), "group", 1)
    ff_own = gathered(ff_mine, "member", 2)
    w_far = [swap(w, "member", 1) for w in w_own]
    ff_far = [swap(f, "member", 1) for f in ff_own]
    extra = [swap(f, "group", k) for k in range(peers, n_group, peers) for f in ff_own]
    extra_far = [swap(f, "member", 1) for f in extra]

    qv = queries(tok_near, tok_gain, w_ref_tok, w_val_tok, where, width)
    qv_far = swap(qv, "member", 1)
    kv_own = keys(lat_near, w_own, w_far, where)
    kv_far = swap(kv_own, "member", 1)

    row_parts = rows_part(qv, kv_own, kv_far, width, n_own, peers)
    row_parts = [row_parts[0]] + [swap(row_parts[k], "group", k) for k in range(1, n_group)]
    pieces = columns(qv, qv_far, kv_own, n_group, n_z, share, width)
    pieces = [pieces[0]] + [swap(pieces[j], "member", 2 * j) for j in range(1, n_z)]
    own_avg = join_members(pieces, where, n_group, share, width)
    avg_near = gathered(own_avg, "group", 1)
    mid, *sends = token_mlp(
        row_parts,
        tok_near[:peers],
        w_out_tok,
        mlp_gain,
        ff_own + extra,
        ff_far + extra_far,
        where,
        ff_share,
    )
    received = [swap(s, "group", k + 1) for k, s in enumerate(sends)]
    lat_cols = from_group(latents, where, width, 1)
    lat_new = latents_part(avg_near, lat_cols, ff_own, ff_far, where, ff_share)
    lat_parts = gathered(lat_new, "group", 1)
    return tuple(finish(mid, received, lat_parts, where))


def solution(mesh):
    in_specs = (
        P(("group", "member"), None),
        P("member", None),
        P(),
        P(),
        P(),
        P(),
        P(),
        P(),
        P("member", None),
        P("member", None),
        P("member", None),
        P(None, "member"),
        P("member", None),
    )
    out_specs = (P(("group", "member"), None), P("member", None))

    return jax.shard_map(per_device, mesh=mesh, in_specs=in_specs, out_specs=out_specs, check_vma=False)
```

profile of v0, /device:TPU:0, one launch (start us, length us, event | category | flops | bytes accessed | tf_op | source)
XLA Modules:
  0.0 129.9 jit_solution(15443412202401356704)
XLA Ops:
  0.6 0.6 pad_add_fusion.refs_0_.pos
  1.2 2.7 %prepare.1 = (bf16[32,1024]{1,0:T(8,128)(2,1)}, bf16[128,512]{1,0:T(8,128)(2,1)}, bf16[160,1024]{1,0:T(8,128)(2,1)}) custom-call(s32[2]{0:T(128)} %pad_add_fusion.refs_0_.pos, bf16[128,1024]{1,0:T(8,128)(2,1)} %lat_ref.1, f32[1,1024]{1,0:T(1,128)} %bitcast.6, bf16[128,1024]{1,0:T(8,128)(2,1)} %ref_w.1, bf16[128,1024]{1,0:T(8,128)(2,1)} %val_w.1, ...), custom_call_target="tpu_custom_call" | custom-call | bytes 4194304 | tf_op jit(solution)/shard_map/prepare/pallas_call | solution.py:171
  3.9 3.1 %collective-permute-start.9 = (bf16[128,512]{1,0:T(8,128)(2,1)}, bf16[128,512]{1,0:T(8,128)(2,1)S(1)}, u32[]{:S(2)}, u32[]{:S(2)}) collective-permute-start(bf16[128,512]{1,0:T(8,128)(2,1)} %get-tuple-element.18.refs_5_), channel_id=1, source_target_pairs={{0,2},{1,3},{2,0},{3,1},{4,6},{5,7},{6,4},{7,5},{8,10},{9,11},{10,... | collective-permute-start | bytes 393224 | tf_op jit(solution)/shard_map/ppermute | solution.py:41
  7.0 3.0 %collective-permute-start.4 = (bf16[32,1024]{1,0:T(8,128)(2,1)}, bf16[32,1024]{1,0:T(8,128)(2,1)S(1)}, u32[]{:S(2)}, u32[]{:S(2)}) collective-permute-start(bf16[32,1024]{1,0:T(8,128)(2,1)} %get-tuple-element.17.refs_0_), channel_id=1, source_target_pairs={{0,4},{1,5},{2,6},{3,7},{4,0},{5,1},{6,2},{7,3},{8,12},{9,13},{10,... | collective-permute-start | bytes 196616 | tf_op jit(solution)/shard_map/ppermute | solution.py:41
  10.1 3.9 %collective-permute-start.5 = (bf16[32,1024]{1,0:T(8,128)(2,1)}, bf16[32,1024]{1,0:T(8,128)(2,1)S(1)}, u32[]{:S(2)}, u32[]{:S(2)}) collective-permute-start(bf16[32,1024]{1,0:T(8,128)(2,1)} %get-tuple-element.17.refs_0_), channel_id=1, source_target_pairs={{0,6},{1,7},{2,4},{3,5},{4,2},{5,3},{6,0},{7,1},{8,14},{9,15},{10,... | collective-permute-start | bytes 196616 | tf_op jit(solution)/shard_map/ppermute | solution.py:41
  14.0 0.7 collective-permute-done.3.refs_1_
  14.7 2.9 %collective-permute-start.11 = (bf16[128,512]{1,0:T(8,128)(2,1)}, bf16[128,512]{1,0:T(8,128)(2,1)S(1)}, u32[]{:S(2)}, u32[]{:S(2)}) collective-permute-start(bf16[128,512]{1,0:T(8,128)(2,1)} %get-tuple-element.18.refs_5_), channel_id=1, source_target_pairs={{0,6},{1,7},{2,4},{3,5},{4,2},{5,3},{6,0},{7,1},{8,14},{9,15},{10,... | collective-permute-start | bytes 393224 | tf_op jit(solution)/shard_map/ppermute | solution.py:41
  17.6 1.5 %collective-permute-start = (bf16[128,1024]{1,0:T(8,128)(2,1)S(1)}, bf16[128,1024]{1,0:T(8,128)(2,1)S(1)}, u32[]{:S(2)}, u32[]{:S(2)}) collective-permute-start(bf16[128,1024]{1,0:T(8,128)(2,1)S(1)} %copy-done.2), channel_id=1, source_target_pairs={{0,8},{8,0},{16,24},{24,16},{1,9},{9,1},{17,25},{25,17},{2,10},{10... | collective-permute-start | bytes 786440 | tf_op jit(solution)/shard_map/ppermute | solution.py:41
  19.1 2.0 %collective-permute-done.5.refs_3_ = bf16[32,1024]{1,0:T(8,128)(2,1)S(1)} collective-permute-done((bf16[32,1024]{1,0:T(8,128)(2,1)}, bf16[32,1024]{1,0:T(8,128)(2,1)S(1)}, u32[]{:S(2)}, u32[]{:S(2)}) %collective-permute-start.5) | collective-permute-done | bytes 65568 | tf_op jit(solution)/shard_map/ppermute | solution.py:41
  21.1 0.5 collective-permute-start.13
  21.7 3.5 %collective-permute-done.10.refs_7_ = bf16[128,512]{1,0:T(8,128)(2,1)S(1)} collective-permute-done((bf16[128,512]{1,0:T(8,128)(2,1)}, bf16[128,512]{1,0:T(8,128)(2,1)S(1)}, u32[]{:S(2)}, u32[]{:S(2)}) %collective-permute-start.10) | collective-permute-done | bytes 131104 | tf_op jit(solution)/shard_map/ppermute | solution.py:41
  25.2 0.5 collective-permute-start.15
  25.7 1.5 %collective-permute-start.1 = (bf16[128,1024]{1,0:T(8,128)(2,1)S(1)}, bf16[128,1024]{1,0:T(8,128)(2,1)S(1)}, u32[]{:S(2)}, u32[]{:S(2)}) collective-permute-start(bf16[128,1024]{1,0:T(8,128)(2,1)S(1)} %copy-done.2), channel_id=1, source_target_pairs={{0,16},{8,24},{16,0},{24,8},{1,17},{9,25},{17,1},{25,9},{2,18},{10... | collective-permute-start | bytes 786440 | tf_op jit(solution)/shard_map/ppermute | solution.py:41
  27.2 0.6 copy-done.13
  27.9 1.4 %collective-permute-start.2 = (bf16[128,1024]{1,0:T(8,128)(2,1)S(1)}, bf16[128,1024]{1,0:T(8,128)(2,1)S(1)}, u32[]{:S(2)}, u32[]{:S(2)}) collective-permute-start(bf16[128,1024]{1,0:T(8,128)(2,1)S(1)} %copy-done.2), channel_id=1, source_target_pairs={{0,24},{8,16},{16,8},{24,0},{1,25},{9,17},{17,9},{25,1},{2,26},{10... | collective-permute-start | bytes 786440 | tf_op jit(solution)/shard_map/ppermute | solution.py:41
  29.3 0.8 copy-done.21
  30.2 0.6 copy-done.15
  30.8 0.5 collective-permute-start.6
  31.4 0.7 copy-done.19
  32.0 1.5 %collective-permute-start.7 = (bf16[128,1024]{1,0:T(8,128)(2,1)S(1)}, bf16[128,1024]{1,0:T(8,128)(2,1)S(1)}, u32[]{:S(2)}, u32[]{:S(2)}) collective-permute-start(bf16[128,1024]{1,0:T(8,128)(2,1)S(1)} %shard_map.140.refs_1_), channel_id=1, source_target_pairs={{0,16},{8,24},{16,0},{24,8},{1,17},{9,25},{17,1},{25,9},{2,18},{10... | collective-permute-start | bytes 786440 | tf_op jit(solution)/shard_map/ppermute | solution.py:41
  33.5 1.4 %collective-permute-start.8 = (bf16[128,1024]{1,0:T(8,128)(2,1)S(1)}, bf16[128,1024]{1,0:T(8,128)(2,1)S(1)}, u32[]{:S(2)}, u32[]{:S(2)}) collective-permute-start(bf16[128,1024]{1,0:T(8,128)(2,1)S(1)} %shard_map.140.refs_1_), channel_id=1, source_target_pairs={{0,24},{8,16},{16,8},{24,0},{1,25},{9,17},{17,9},{25,1},{2,26},{10... | collective-permute-start | bytes 786440 | tf_op jit(solution)/shard_map/ppermute | solution.py:41
  35.0 5.5 %collective-permute-done.1.refs_3_.refs_9_ = bf16[128,1024]{1,0:T(8,128)(2,1)S(1)} collective-permute-done((bf16[128,1024]{1,0:T(8,128)(2,1)S(1)}, bf16[128,1024]{1,0:T(8,128)(2,1)S(1)}, u32[]{:S(2)}, u32[]{:S(2)}) %collective-permute-start.1) | collective-permute-done | bytes 262176 | tf_op jit(solution)/shard_map/ppermute | solution.py:41
  40.5 3.1 %collective-permute-start.20 = (bf16[160,1024]{1,0:T(8,128)(2,1)}, bf16[160,1024]{1,0:T(8,128)(2,1)S(1)}, u32[]{:S(2)}, u32[]{:S(2)}) collective-permute-start(bf16[160,1024]{1,0:T(8,128)(2,1)} %get-tuple-element.23.refs_11_.refs_6_), channel_id=1, source_target_pairs={{0,2},{1,3},{2,0},{3,1},{4,6},{5,7},{6,4},{7,5},{8,10},{9,11},{10,... | collective-permute-start | bytes 983048 | tf_op jit(solution)/shard_map/ppermute | solution.py:41
  43.6 1.3 %collective-permute-start.21 = (bf16[160,1024]{1,0:T(8,128)(2,1)}, bf16[160,1024]{1,0:T(8,128)(2,1)S(1)}, u32[]{:S(2)}, u32[]{:S(2)}) collective-permute-start(bf16[160,1024]{1,0:T(8,128)(2,1)} %get-tuple-element.23.refs_11_.refs_6_), channel_id=1, source_target_pairs={{0,4},{1,5},{2,6},{3,7},{4,0},{5,1},{6,2},{7,3},{8,12},{9,13},{10,... | collective-permute-start | bytes 983048 | tf_op jit(solution)/shard_map/ppermute | solution.py:41
  45.0 4.0 %queries.1.q_ref.own = bf16[512,512]{1,0:T(8,128)(2,1)} custom-call(s32[2]{0:T(128)} %pad_add_fusion.refs_0_.pos, bf16[128,1024]{1,0:T(8,128)(2,1)} %refs_7_.3, bf16[128,1024]{1,0:T(8,128)(2,1)} %copy-done.4, bf16[128,1024]{1,0:T(8,128)(2,1)} %copy-done.6, bf16[128,1024]{1,0:T(8,128)(2,1)} %copy-done.8, f32[1,1024]{1,0:T(1,128)} %bitcast.7, ...), custom_call_target="tpu_custom_call" | custom-call | flops 536870912 | bytes 2097152 | tf_op jit(solution)/shard_map/queries/pallas_call | solution.py:109
  49.0 0.1 collective-permute-start.30
  49.1 1.7 %collective-permute-done.7.refs_3_ = bf16[128,1024]{1,0:T(8,128)(2,1)S(1)} collective-permute-done((bf16[128,1024]{1,0:T(8,128)(2,1)S(1)}, bf16[128,1024]{1,0:T(8,128)(2,1)S(1)}, u32[]{:S(2)}, u32[]{:S(2)}) %collective-permute-start.7) | collective-permute-done | bytes 262176 | tf_op jit(solution)/shard_map/ppermute | solution.py:41
  50.9 0.9 copy-done.12
  51.8 0.9 copy-done.20
  52.7 1.3 %shard_map.141.own.k_ref = bf16[512,512]{1,0:T(8,128)(2,1)S(1)} custom-call(s32[2]{0:T(128)S(1)} %copy-done.22, bf16[128,1024]{1,0:T(8,128)(2,1)S(1)} %shard_map.140.refs_1_, bf16[128,1024]{1,0:T(8,128)(2,1)S(1)} %collective-permute-done.6.refs_2_, bf16[128,1024]{1,0:T(8,128)(2,1)S(1)} %collective-permute-done.7.refs_3_, ...), custom_call_target="tpu_custom_call" | custom-call | flops 536870912 | bytes 2621448 | tf_op jit(solution)/shard_map/pallas_call | solution.py:53
  54.0 0.1 collective-permute-start.16
  54.1 2.7 %collective-permute-start.22 = (bf16[160,1024]{1,0:T(8,128)(2,1)S(1)}, bf16[160,1024]{1,0:T(8,128)(2,1)S(1)}, u32[]{:S(2)}, u32[]{:S(2)}) collective-permute-start(bf16[160,1024]{1,0:T(8,128)(2,1)S(1)} %copy-done.1), channel_id=1, source_target_pairs={{0,6},{1,7},{2,4},{3,5},{4,2},{5,3},{6,0},{7,1},{8,14},{9,15},{10,... | collective-permute-start | bytes 983048 | tf_op jit(solution)/shard_map/ppermute | solution.py:41
  56.7 1.0 collective-permute-done.20.refs_12_.refs_7_
  57.8 0.5 collective-permute-start.24
  58.3 9.0 %collective-permute-done.22.refs_14_.refs_9_ = bf16[160,1024]{1,0:T(8,128)(2,1)S(1)} collective-permute-done((bf16[160,1024]{1,0:T(8,128)(2,1)S(1)}, bf16[160,1024]{1,0:T(8,128)(2,1)S(1)}, u32[]{:S(2)}, u32[]{:S(2)}) %collective-permute-start.22) | collective-permute-done | bytes 327712 | tf_op jit(solution)/shard_map/ppermute | solution.py:41
  67.3 0.5 collective-permute-start.26
  67.8 3.7 %shard_map.144 = (bf16[128,384]{1,0:T(8,128)(2,1)S(1)}, bf16[128,384]{1,0:T(8,128)(2,1)S(1)}, bf16[128,384]{1,0:T(8,128)(2,1)S(1)}, bf16[128,384]{1,0:T(8,128)(2,1)S(1)}) custom-call(bf16[512,512]{1,0:T(8,128)(2,1)S(1)} %copy-done, bf16[512,512]{1,0:T(8,128)(2,1)S(1)} %collective-permute-done.30.far, bf16[512,512]{1,0:T(8,128)(2,1)S(1)} %shard_map.141.own.k_ref), custom_call_target="tpu_custom_call" | custom-call | flops 1073741824 | bytes 1966080 | tf_op jit(solution)/shard_map/pallas_call | solution.py:53
  71.6 7.6 %collective-permute-start.31 = (bf16[128,384]{1,0:T(8,128)(2,1)S(1)}, bf16[128,384]{1,0:T(8,128)(2,1)S(1)}, u32[]{:S(2)}, u32[]{:S(2)}) collective-permute-start(bf16[128,384]{1,0:T(8,128)(2,1)S(1)} %get-tuple-element.29), channel_id=1, source_target_pairs={{0,2},{1,3},{2,0},{3,1},{4,6},{5,7},{6,4},{7,5},{8,10},{9,11},{10,... | collective-permute-start | bytes 294920 | tf_op jit(solution)/shard_map/ppermute | solution.py:41
  79.1 1.3 %collective-permute-start.32 = (bf16[128,384]{1,0:T(8,128)(2,1)S(1)}, bf16[128,384]{1,0:T(8,128)(2,1)S(1)}, u32[]{:S(2)}, u32[]{:S(2)}) collective-permute-start(bf16[128,384]{1,0:T(8,128)(2,1)S(1)} %get-tuple-element.30), channel_id=1, source_target_pairs={{0,4},{1,5},{2,6},{3,7},{4,0},{5,1},{6,2},{7,3},{8,12},{9,13},{10,... | collective-permute-start | bytes 294920 | tf_op jit(solution)/shard_map/ppermute | solution.py:41
  80.5 1.5 %collective-permute-start.33 = (bf16[128,384]{1,0:T(8,128)(2,1)S(1)}, bf16[128,384]{1,0:T(8,128)(2,1)S(1)}, u32[]{:S(2)}, u32[]{:S(2)}) collective-permute-start(bf16[128,384]{1,0:T(8,128)(2,1)S(1)} %get-tuple-element.31), channel_id=1, source_target_pairs={{0,6},{1,7},{2,4},{3,5},{4,2},{5,3},{6,0},{7,1},{8,14},{9,15},{10,... | collective-permute-start | bytes 294920 | tf_op jit(solution)/shard_map/ppermute | solution.py:41
  81.9 3.6 %shard_map.142 = (bf16[512,256]{1,0:T(8,128)(2,1)S(1)}, bf16[512,256]{1,0:T(8,128)(2,1)S(1)}, bf16[512,256]{1,0:T(8,128)(2,1)S(1)}, bf16[512,256]{1,0:T(8,128)(2,1)S(1)}) custom-call(bf16[512,512]{1,0:T(8,128)(2,1)S(1)} %copy-done, bf16[512,512]{1,0:T(8,128)(2,1)S(1)} %shard_map.141.own.k_ref, bf16[512,512]{1,0:T(8,128)(2,1)S(1)} %collective-permute-done.16.far), custom_call_target="tpu_custom_call" | custom-call | flops 1073741824 | bytes 2621440 | tf_op jit(solution)/shard_map/pallas_call | solution.py:53
  85.6 1.6 %collective-permute-start.17 = (bf16[512,256]{1,0:T(8,128)(2,1)S(1)}, bf16[512,256]{1,0:T(8,128)(2,1)S(1)}, u32[]{:S(2)}, u32[]{:S(2)}) collective-permute-start(bf16[512,256]{1,0:T(8,128)(2,1)S(1)} %get-tuple-element.20), channel_id=1, source_target_pairs={{0,8},{8,0},{16,24},{24,16},{1,9},{9,1},{17,25},{25,17},{2,10},{10... | collective-permute-start | bytes 786440 | tf_op jit(solution)/shard_map/ppermute | solution.py:41
  87.2 2.5 %collective-permute-done.32.refs_3_ = bf16[128,384]{1,0:T(8,128)(2,1)S(1)} collective-permute-done((bf16[128,384]{1,0:T(8,128)(2,1)S(1)}, bf16[128,384]{1,0:T(8,128)(2,1)S(1)}, u32[]{:S(2)}, u32[]{:S(2)}) %collective-permute-start.32) | collective-permute-done | bytes 98336 | tf_op jit(solution)/shard_map/ppermute | solution.py:41
  89.7 1.7 %collective-permute-start.18 = (bf16[512,256]{1,0:T(8,128)(2,1)S(1)}, bf16[512,256]{1,0:T(8,128)(2,1)S(1)}, u32[]{:S(2)}, u32[]{:S(2)}) collective-permute-start(bf16[512,256]{1,0:T(8,128)(2,1)S(1)} %get-tuple-element.21), channel_id=1, source_target_pairs={{0,16},{8,24},{16,0},{24,8},{1,17},{9,25},{17,1},{25,9},{2,18},{10... | collective-permute-start | bytes 786440 | tf_op jit(solution)/shard_map/ppermute | solution.py:41
  91.3 1.4 %collective-permute-start.19 = (bf16[512,256]{1,0:T(8,128)(2,1)S(1)}, bf16[512,256]{1,0:T(8,128)(2,1)S(1)}, u32[]{:S(2)}, u32[]{:S(2)}) collective-permute-start(bf16[512,256]{1,0:T(8,128)(2,1)S(1)} %get-tuple-element.22), channel_id=1, source_target_pairs={{0,24},{8,16},{16,8},{24,0},{1,25},{9,17},{17,9},{25,1},{2,26},{10... | collective-permute-start | bytes 786440 | tf_op jit(solution)/shard_map/ppermute | solution.py:41
  92.8 1.5 %shard_map.145.refs_1_ = f32[128,256]{1,0:T(8,128)S(1)} custom-call(s32[2]{0:T(128)S(1)} %copy-done.22, bf16[128,384]{1,0:T(8,128)(2,1)S(1)} %get-tuple-element.28.refs_1_, bf16[128,384]{1,0:T(8,128)(2,1)S(1)} %collective-permute-done.31.refs_2_, bf16[128,384]{1,0:T(8,128)(2,1)S(1)} %collective-permute-done.32.refs_3_, ...), custom_call_target="tpu_custom_call" | custom-call | bytes 524296 | tf_op jit(solution)/shard_map/pallas_call | solution.py:53
  94.3 0.5 collective-permute-start.34
  94.7 1.7 %collective-permute-start.35 = (f32[128,256]{1,0:T(8,128)S(1)}, f32[128,256]{1,0:T(8,128)}, u32[]{:S(2)}, u32[]{:S(2)}) collective-permute-start(f32[128,256]{1,0:T(8,128)S(1)} %shard_map.145.refs_1_), channel_id=1, source_target_pairs={{0,16},{8,24},{16,0},{24,8},{1,17},{9,25},{17,1},{25,9},{2,18},{10... | collective-permute-start | bytes 393224 | tf_op jit(solution)/shard_map/ppermute | solution.py:41
  96.4 1.4 %collective-permute-start.36 = (f32[128,256]{1,0:T(8,128)S(1)}, f32[128,256]{1,0:T(8,128)}, u32[]{:S(2)}, u32[]{:S(2)}) collective-permute-start(f32[128,256]{1,0:T(8,128)S(1)} %shard_map.145.refs_1_), channel_id=1, source_target_pairs={{0,24},{8,16},{16,8},{24,0},{1,25},{9,17},{17,9},{25,1},{2,26},{10... | collective-permute-start | bytes 393224 | tf_op jit(solution)/shard_map/ppermute | solution.py:41
  97.8 7.8 %collective-permute-done.18.refs_5_ = bf16[512,256]{1,0:T(8,128)(2,1)S(1)} collective-permute-done((bf16[512,256]{1,0:T(8,128)(2,1)S(1)}, bf16[512,256]{1,0:T(8,128)(2,1)S(1)}, u32[]{:S(2)}, u32[]{:S(2)}) %collective-permute-start.18) | collective-permute-done | bytes 262176 | tf_op jit(solution)/shard_map/ppermute | solution.py:41
  105.7 5.5 %shard_map.143 = (f32[128,1024]{1,0:T(8,128)S(1)}, bf16[128,1024]{1,0:T(8,128)(2,1)}, bf16[128,1024]{1,0:T(8,128)(2,1)}, bf16[128,1024]{1,0:T(8,128)(2,1)}) custom-call(s32[2]{0:T(128)S(1)} %copy-done.22, bf16[1024,1024]{1,0:T(8,128)(2,1)} %refs_1_.3, f32[1,1024]{1,0:T(1,128)S(1)} %bitcast.5, bf16[512,256]{1,0:T(8,128)(2,1)S(1)} %get-tuple-element.19.refs_3_, ...), custom_call_target="tpu_custom_call" | custom-call | flops 2147483648 | bytes 8130568 | tf_op jit(solution)/shard_map/pallas_call | solution.py:53
  111.2 1.6 %collective-permute-start.27 = (bf16[128,1024]{1,0:T(8,128)(2,1)}, bf16[128,1024]{1,0:T(8,128)(2,1)S(1)}, u32[]{:S(2)}, u32[]{:S(2)}) collective-permute-start(bf16[128,1024]{1,0:T(8,128)(2,1)} %get-tuple-element.25), channel_id=1, source_target_pairs={{0,8},{8,0},{16,24},{24,16},{1,9},{9,1},{17,25},{25,17},{2,10},{10... | collective-permute-start | bytes 786440 | tf_op jit(solution)/shard_map/ppermute | solution.py:41
  112.8 1.0 collective-permute-start.28
  113.8 0.6 copy-done.17
  114.4 0.9 collective-permute-start.29
  115.3 0.8 constant_dynamic-slice_fusion.refs_5_
  116.2 0.9 copy-done.18
  117.1 1.3 %shard_map.146.refs_5_ = bf16[128,256]{1,0:T(8,128)(2,1)S(1)} custom-call(s32[2]{0:T(128)S(1)} %copy-done.22, f32[128,256]{1,0:T(8,128)S(1)} %shard_map.145.refs_1_, f32[128,256]{1,0:T(8,128)S(1)} %copy-done.18, f32[128,256]{1,0:T(8,128)} %collective-permute-done.35.refs_3_, f32[128,256]{1,0:T(8,128)} %collective-permute-done.36.refs_4_, ...), custom_call_target="tpu_custom_call" | custom-call | flops 67108864 | bytes 3276808 | tf_op jit(solution)/shard_map/pallas_call | solution.py:53
  118.5 1.6 %collective-permute-start.37 = (bf16[128,256]{1,0:T(8,128)(2,1)S(1)}, bf16[128,256]{1,0:T(8,128)(2,1)S(1)}, u32[]{:S(2)}, u32[]{:S(2)}) collective-permute-start(bf16[128,256]{1,0:T(8,128)(2,1)S(1)} %shard_map.146.refs_5_), channel_id=1, source_target_pairs={{0,8},{8,0},{16,24},{24,16},{1,9},{9,1},{17,25},{25,17},{2,10},{10... | collective-permute-start | bytes 196616 | tf_op jit(solution)/shard_map/ppermute | solution.py:41
  120.1 1.0 collective-permute-start.38
  121.1 1.7 %collective-permute-done.37.refs_6_ = bf16[128,256]{1,0:T(8,128)(2,1)S(1)} collective-permute-done((bf16[128,256]{1,0:T(8,128)(2,1)S(1)}, bf16[128,256]{1,0:T(8,128)(2,1)S(1)}, u32[]{:S(2)}, u32[]{:S(2)}) %collective-permute-start.37) | collective-permute-done | bytes 65568 | tf_op jit(solution)/shard_map/ppermute | solution.py:41
  122.8 2.0 %collective-permute-start.39 = (bf16[128,256]{1,0:T(8,128)(2,1)S(1)}, bf16[128,256]{1,0:T(8,128)(2,1)S(1)}, u32[]{:S(2)}, u32[]{:S(2)}) collective-permute-start(bf16[128,256]{1,0:T(8,128)(2,1)S(1)} %shard_map.146.refs_5_), channel_id=1, source_target_pairs={{0,24},{8,16},{16,8},{24,0},{1,25},{9,17},{17,9},{25,1},{2,26},{10... | collective-permute-start | bytes 196616 | tf_op jit(solution)/shard_map/ppermute | solution.py:41
  124.8 3.1 %collective-permute-done.39.refs_8_ = bf16[128,256]{1,0:T(8,128)(2,1)S(1)} collective-permute-done((bf16[128,256]{1,0:T(8,128)(2,1)S(1)}, bf16[128,256]{1,0:T(8,128)(2,1)S(1)}, u32[]{:S(2)}, u32[]{:S(2)}) %collective-permute-start.39) | collective-permute-done | bytes 65568 | tf_op jit(solution)/shard_map/ppermute | solution.py:41
  128.0 1.9 %shard_map.147 = (bf16[128,1024]{1,0:T(8,128)(2,1)}, bf16[128,1024]{1,0:T(8,128)(2,1)}) custom-call(s32[2]{0:T(128)S(1)} %copy-done.22, f32[128,1024]{1,0:T(8,128)S(1)} %get-tuple-element.24.refs_1_, bf16[128,1024]{1,0:T(8,128)(2,1)S(1)} %collective-permute-done.27.refs_2_, bf16[128,1024]{1,0:T(8,128)(2,1)} %collective-permute-done.28.refs_3_, ...), custom_call_target="tpu_custom_call" | custom-call | bytes 2097160 | tf_op jit(solution)/shard_map/pallas_call | solution.py:53
  (76 shorter events, 0.2 us)
Async XLA Ops:
  0.6 17.0 %copy-start.2 = (bf16[128,1024]{1,0:T(8,128)(2,1)S(1)}, bf16[128,1024]{1,0:T(8,128)(2,1)}, u32[]{:S(2)}) copy-start(bf16[128,1024]{1,0:T(8,128)(2,1)} %refs_7_.3) | copy-start | bytes 786436
  3.9 17.2 %collective-permute-start.9 = (bf16[128,512]{1,0:T(8,128)(2,1)}, bf16[128,512]{1,0:T(8,128)(2,1)S(1)}, u32[]{:S(2)}, u32[]{:S(2)}) collective-permute-start(bf16[128,512]{1,0:T(8,128)(2,1)} %get-tuple-element.18.refs_5_), channel_id=1, source_target_pairs={{0,2},{1,3},{2,0},{3,1},{4,6},{5,7},{6,4},{7,5},{8,10},{9,11},{10,... | collective-permute-start | bytes 393224 | tf_op jit(solution)/shard_map/ppermute | solution.py:41
  7.0 7.7 %collective-permute-start.3 = (bf16[32,1024]{1,0:T(8,128)(2,1)}, bf16[32,1024]{1,0:T(8,128)(2,1)S(1)}, u32[]{:S(2)}, u32[]{:S(2)}) collective-permute-start(bf16[32,1024]{1,0:T(8,128)(2,1)} %get-tuple-element.17.refs_0_), channel_id=1, source_target_pairs={{0,2},{1,3},{2,0},{3,1},{4,6},{5,7},{6,4},{7,5},{8,10},{9,11},{10,... | collective-permute-start | bytes 196616 | tf_op jit(solution)/shard_map/ppermute | solution.py:41
  7.0 10.6 %collective-permute-start.4 = (bf16[32,1024]{1,0:T(8,128)(2,1)}, bf16[32,1024]{1,0:T(8,128)(2,1)S(1)}, u32[]{:S(2)}, u32[]{:S(2)}) collective-permute-start(bf16[32,1024]{1,0:T(8,128)(2,1)} %get-tuple-element.17.refs_0_), channel_id=1, source_target_pairs={{0,4},{1,5},{2,6},{3,7},{4,0},{5,1},{6,2},{7,3},{8,12},{9,13},{10,... | collective-permute-start | bytes 196616 | tf_op jit(solution)/shard_map/ppermute | solution.py:41
  10.0 15.1 %collective-permute-start.10 = (bf16[128,512]{1,0:T(8,128)(2,1)}, bf16[128,512]{1,0:T(8,128)(2,1)S(1)}, u32[]{:S(2)}, u32[]{:S(2)}) collective-permute-start(bf16[128,512]{1,0:T(8,128)(2,1)} %get-tuple-element.18.refs_5_), channel_id=1, source_target_pairs={{0,4},{1,5},{2,6},{3,7},{4,0},{5,1},{6,2},{7,3},{8,12},{9,13},{10,... | collective-permute-start | bytes 393224 | tf_op jit(solution)/shard_map/ppermute | solution.py:41
  10.1 11.1 %collective-permute-start.5 = (bf16[32,1024]{1,0:T(8,128)(2,1)}, bf16[32,1024]{1,0:T(8,128)(2,1)S(1)}, u32[]{:S(2)}, u32[]{:S(2)}) collective-permute-start(bf16[32,1024]{1,0:T(8,128)(2,1)} %get-tuple-element.17.refs_0_), channel_id=1, source_target_pairs={{0,6},{1,7},{2,4},{3,5},{4,2},{5,3},{6,0},{7,1},{8,14},{9,15},{10,... | collective-permute-start | bytes 196616 | tf_op jit(solution)/shard_map/ppermute | solution.py:41
  14.7 10.5 %collective-permute-start.11 = (bf16[128,512]{1,0:T(8,128)(2,1)}, bf16[128,512]{1,0:T(8,128)(2,1)S(1)}, u32[]{:S(2)}, u32[]{:S(2)}) collective-permute-start(bf16[128,512]{1,0:T(8,128)(2,1)} %get-tuple-element.18.refs_5_), channel_id=1, source_target_pairs={{0,6},{1,7},{2,4},{3,5},{4,2},{5,3},{6,0},{7,1},{8,14},{9,15},{10,... | collective-permute-start | bytes 393224 | tf_op jit(solution)/shard_map/ppermute | solution.py:41
  17.6 15.9 %collective-permute-start = (bf16[128,1024]{1,0:T(8,128)(2,1)S(1)}, bf16[128,1024]{1,0:T(8,128)(2,1)S(1)}, u32[]{:S(2)}, u32[]{:S(2)}) collective-permute-start(bf16[128,1024]{1,0:T(8,128)(2,1)S(1)} %copy-done.2), channel_id=1, source_target_pairs={{0,8},{8,0},{16,24},{24,16},{1,9},{9,1},{17,25},{25,17},{2,10},{10... | collective-permute-start | bytes 786440 | tf_op jit(solution)/shard_map/ppermute | solution.py:41
  21.1 4.5 %collective-permute-start.12 = (bf16[128,512]{1,0:T(8,128)(2,1)}, bf16[128,512]{1,0:T(8,128)(2,1)S(1)}, u32[]{:S(2)}, u32[]{:S(2)}) collective-permute-start(bf16[128,512]{1,0:T(8,128)(2,1)} %get-tuple-element.18.refs_5_), channel_id=1, source_target_pairs={{0,1},{1,0},{2,3},{3,2},{4,5},{5,4},{6,7},{7,6},{8,9},{9,8},{10,11... | collective-permute-start | bytes 393224 | tf_op jit(solution)/shard_map/ppermute | solution.py:41
  21.1 6.1 %collective-permute-start.13 = (bf16[128,512]{1,0:T(8,128)(2,1)S(1)}, bf16[128,512]{1,0:T(8,128)(2,1)S(1)}, u32[]{:S(2)}, u32[]{:S(2)}) collective-permute-start(bf16[128,512]{1,0:T(8,128)(2,1)S(1)} %collective-permute-done.9.refs_6_), channel_id=1, source_target_pairs={{0,1},{1,0},{2,3},{3,2},{4,5},{5,4},{6,7},{7,6},{8,9},{9,8},{10,11... | collective-permute-start | bytes 393224 | tf_op jit(solution)/shard_map/ppermute | solution.py:41
  25.2 5.0 %collective-permute-start.14 = (bf16[128,512]{1,0:T(8,128)(2,1)S(1)}, bf16[128,512]{1,0:T(8,128)(2,1)S(1)}, u32[]{:S(2)}, u32[]{:S(2)}) collective-permute-start(bf16[128,512]{1,0:T(8,128)(2,1)S(1)} %collective-permute-done.10.refs_7_), channel_id=1, source_target_pairs={{0,1},{1,0},{2,3},{3,2},{4,5},{5,4},{6,7},{7,6},{8,9},{9,8},{10,11... | collective-permute-start | bytes 393224 | tf_op jit(solution)/shard_map/ppermute | solution.py:41
  25.2 6.2 %collective-permute-start.15 = (bf16[128,512]{1,0:T(8,128)(2,1)S(1)}, bf16[128,512]{1,0:T(8,128)(2,1)S(1)}, u32[]{:S(2)}, u32[]{:S(2)}) collective-permute-start(bf16[128,512]{1,0:T(8,128)(2,1)S(1)} %collective-permute-done.11.refs_8_), channel_id=1, source_target_pairs={{0,1},{1,0},{2,3},{3,2},{4,5},{5,4},{6,7},{7,6},{8,9},{9,8},{10,11... | collective-permute-start | bytes 393224 | tf_op jit(solution)/shard_map/ppermute | solution.py:41
  25.7 19.3 %copy-start.11 = (bf16[128,512]{1,0:T(8,128)(2,1)}, bf16[128,512]{1,0:T(8,128)(2,1)S(1)}, u32[]{:S(2)}) copy-start(bf16[128,512]{1,0:T(8,128)(2,1)S(1)} %collective-permute-done.12.refs_9_) | copy-start | bytes 393220
  25.7 14.8 %collective-permute-start.1 = (bf16[128,1024]{1,0:T(8,128)(2,1)S(1)}, bf16[128,1024]{1,0:T(8,128)(2,1)S(1)}, u32[]{:S(2)}, u32[]{:S(2)}) collective-permute-start(bf16[128,1024]{1,0:T(8,128)(2,1)S(1)} %copy-done.2), channel_id=1, source_target_pairs={{0,16},{8,24},{16,0},{24,8},{1,17},{9,25},{17,1},{25,9},{2,18},{10... | collective-permute-start | bytes 786440 | tf_op jit(solution)/shard_map/ppermute | solution.py:41
  27.2 0.6 copy-start.13
  27.9 15.8 %collective-permute-start.2 = (bf16[128,1024]{1,0:T(8,128)(2,1)S(1)}, bf16[128,1024]{1,0:T(8,128)(2,1)S(1)}, u32[]{:S(2)}, u32[]{:S(2)}) collective-permute-start(bf16[128,1024]{1,0:T(8,128)(2,1)S(1)} %copy-done.2), channel_id=1, source_target_pairs={{0,24},{8,16},{16,8},{24,0},{1,25},{9,17},{17,9},{25,1},{2,26},{10... | collective-permute-start | bytes 786440 | tf_op jit(solution)/shard_map/ppermute | solution.py:41
  29.3 0.8 copy-start.21
  30.2 0.7 copy-start.15
  30.8 18.2 %collective-permute-start.6 = (bf16[128,1024]{1,0:T(8,128)(2,1)S(1)}, bf16[128,1024]{1,0:T(8,128)(2,1)S(1)}, u32[]{:S(2)}, u32[]{:S(2)}) collective-permute-start(bf16[128,1024]{1,0:T(8,128)(2,1)S(1)} %shard_map.140.refs_1_), channel_id=1, source_target_pairs={{0,8},{8,0},{16,24},{24,16},{1,9},{9,1},{17,25},{25,17},{2,10},{10... | collective-permute-start | bytes 786440 | tf_op jit(solution)/shard_map/ppermute | solution.py:41
  31.4 0.7 copy-start.19
  32.0 18.8 %collective-permute-start.7 = (bf16[128,1024]{1,0:T(8,128)(2,1)S(1)}, bf16[128,1024]{1,0:T(8,128)(2,1)S(1)}, u32[]{:S(2)}, u32[]{:S(2)}) collective-permute-start(bf16[128,1024]{1,0:T(8,128)(2,1)S(1)} %shard_map.140.refs_1_), channel_id=1, source_target_pairs={{0,16},{8,24},{16,0},{24,8},{1,17},{9,25},{17,1},{25,9},{2,18},{10... | collective-permute-start | bytes 786440 | tf_op jit(solution)/shard_map/ppermute | solution.py:41
  33.5 11.4 %copy-start.4 = (bf16[128,1024]{1,0:T(8,128)(2,1)}, bf16[128,1024]{1,0:T(8,128)(2,1)S(1)}, u32[]{:S(2)}) copy-start(bf16[128,1024]{1,0:T(8,128)(2,1)S(1)} %collective-permute-done.refs_2_.refs_8_) | copy-start | bytes 786436
  33.5 17.3 %collective-permute-start.8 = (bf16[128,1024]{1,0:T(8,128)(2,1)S(1)}, bf16[128,1024]{1,0:T(8,128)(2,1)S(1)}, u32[]{:S(2)}, u32[]{:S(2)}) collective-permute-start(bf16[128,1024]{1,0:T(8,128)(2,1)S(1)} %shard_map.140.refs_1_), channel_id=1, source_target_pairs={{0,24},{8,16},{16,8},{24,0},{1,25},{9,17},{17,9},{25,1},{2,26},{10... | collective-permute-start | bytes 786440 | tf_op jit(solution)/shard_map/ppermute | solution.py:41
  40.5 4.5 %copy-start.6 = (bf16[128,1024]{1,0:T(8,128)(2,1)}, bf16[128,1024]{1,0:T(8,128)(2,1)S(1)}, u32[]{:S(2)}) copy-start(bf16[128,1024]{1,0:T(8,128)(2,1)S(1)} %collective-permute-done.1.refs_3_.refs_9_) | copy-start | bytes 786436
  40.5 17.3 %collective-permute-start.20 = (bf16[160,1024]{1,0:T(8,128)(2,1)}, bf16[160,1024]{1,0:T(8,128)(2,1)S(1)}, u32[]{:S(2)}, u32[]{:S(2)}) collective-permute-start(bf16[160,1024]{1,0:T(8,128)(2,1)} %get-tuple-element.23.refs_11_.refs_6_), channel_id=1, source_target_pairs={{0,2},{1,3},{2,0},{3,1},{4,6},{5,7},{6,4},{7,5},{8,10},{9,11},{10,... | collective-permute-start | bytes 983048 | tf_op jit(solution)/shard_map/ppermute | solution.py:41
  43.6 1.3 %copy-start.8 = (bf16[128,1024]{1,0:T(8,128)(2,1)}, bf16[128,1024]{1,0:T(8,128)(2,1)S(1)}, u32[]{:S(2)}) copy-start(bf16[128,1024]{1,0:T(8,128)(2,1)S(1)} %collective-permute-done.2.refs_4_.refs_10_) | copy-start | bytes 786436
  43.6 14.2 %collective-permute-start.21 = (bf16[160,1024]{1,0:T(8,128)(2,1)}, bf16[160,1024]{1,0:T(8,128)(2,1)S(1)}, u32[]{:S(2)}, u32[]{:S(2)}) collective-permute-start(bf16[160,1024]{1,0:T(8,128)(2,1)} %get-tuple-element.23.refs_11_.refs_6_), channel_id=1, source_target_pairs={{0,4},{1,5},{2,6},{3,7},{4,0},{5,1},{6,2},{7,3},{8,12},{9,13},{10,... | collective-permute-start | bytes 983048 | tf_op jit(solution)/shard_map/ppermute | solution.py:41
  45.0 5.9 %copy-start.10 = (bf16[128,512]{1,0:T(8,128)(2,1)S(1)}, bf16[128,512]{1,0:T(8,128)(2,1)}, u32[]{:S(2)}) copy-start(bf16[128,512]{1,0:T(8,128)(2,1)} %get-tuple-element.18.refs_5_) | copy-start | bytes 393220
  45.0 5.9 %copy-start.14 = (bf16[128,512]{1,0:T(8,128)(2,1)S(1)}, bf16[128,512]{1,0:T(8,128)(2,1)}, u32[]{:S(2)}) copy-start(bf16[128,512]{1,0:T(8,128)(2,1)} %copy-done.13) | copy-start | bytes 393220
  45.0 5.9 %copy-start.16 = (bf16[128,512]{1,0:T(8,128)(2,1)S(1)}, bf16[128,512]{1,0:T(8,128)(2,1)}, u32[]{:S(2)}) copy-start(bf16[128,512]{1,0:T(8,128)(2,1)} %copy-done.15) | copy-start | bytes 393220
  45.0 5.9 %copy-start.22 = (s32[2]{0:T(128)S(1)}, s32[2]{0:T(128)}, u32[]{:S(2)}) copy-start(s32[2]{0:T(128)} %pad_add_fusion.refs_0_.pos) | copy-start | bytes 28
  49.0 5.1 %copy-start.1 = (bf16[160,1024]{1,0:T(8,128)(2,1)S(1)}, bf16[160,1024]{1,0:T(8,128)(2,1)}, u32[]{:S(2)}) copy-start(bf16[160,1024]{1,0:T(8,128)(2,1)} %get-tuple-element.23.refs_11_.refs_6_) | copy-start | bytes 983044
  49.0 18.8 %copy-start = (bf16[512,512]{1,0:T(8,128)(2,1)S(1)}, bf16[512,512]{1,0:T(8,128)(2,1)}, u32[]{:S(2)}) copy-start(bf16[512,512]{1,0:T(8,128)(2,1)} %queries.1.q_ref.own) | copy-start | bytes 1572868
  49.0 18.3 %collective-permute-start.30 = (bf16[512,512]{1,0:T(8,128)(2,1)}, bf16[512,512]{1,0:T(8,128)(2,1)S(1)}, u32[]{:S(2)}, u32[]{:S(2)}) collective-permute-start(bf16[512,512]{1,0:T(8,128)(2,1)} %queries.1.q_ref.own), channel_id=1, source_target_pairs={{0,1},{1,0},{2,3},{3,2},{4,5},{5,4},{6,7},{7,6},{8,9},{9,8},{10,11... | collective-permute-start | bytes 1572872 | tf_op jit(solution)/shard_map/ppermute | solution.py:41
  50.9 0.9 copy-start.12
  51.8 0.9 copy-start.20
  54.0 26.4 %collective-permute-start.16 = (bf16[512,512]{1,0:T(8,128)(2,1)S(1)}, bf16[512,512]{1,0:T(8,128)(2,1)S(1)}, u32[]{:S(2)}, u32[]{:S(2)}) collective-permute-start(bf16[512,512]{1,0:T(8,128)(2,1)S(1)} %shard_map.141.own.k_ref), channel_id=1, source_target_pairs={{0,1},{1,0},{2,3},{3,2},{4,5},{5,4},{6,7},{7,6},{8,9},{9,8},{10,11... | collective-permute-start | bytes 1572872 | tf_op jit(solution)/shard_map/ppermute | solution.py:41
  54.1 13.2 %collective-permute-start.22 = (bf16[160,1024]{1,0:T(8,128)(2,1)S(1)}, bf16[160,1024]{1,0:T(8,128)(2,1)S(1)}, u32[]{:S(2)}, u32[]{:S(2)}) collective-permute-start(bf16[160,1024]{1,0:T(8,128)(2,1)S(1)} %copy-done.1), channel_id=1, source_target_pairs={{0,6},{1,7},{2,4},{3,5},{4,2},{5,3},{6,0},{7,1},{8,14},{9,15},{10,... | collective-permute-start | bytes 983048 | tf_op jit(solution)/shard_map/ppermute | solution.py:41
  57.8 13.8 %collective-permute-start.23 = (bf16[160,1024]{1,0:T(8,128)(2,1)S(1)}, bf16[160,1024]{1,0:T(8,128)(2,1)S(1)}, u32[]{:S(2)}, u32[]{:S(2)}) collective-permute-start(bf16[160,1024]{1,0:T(8,128)(2,1)S(1)} %copy-done.1), channel_id=1, source_target_pairs={{0,1},{1,0},{2,3},{3,2},{4,5},{5,4},{6,7},{7,6},{8,9},{9,8},{10,11... | collective-permute-start | bytes 983048 | tf_op jit(solution)/shard_map/ppermute | solution.py:41
  57.8 21.3 %collective-permute-start.24 = (bf16[160,1024]{1,0:T(8,128)(2,1)S(1)}, bf16[160,1024]{1,0:T(8,128)(2,1)S(1)}, u32[]{:S(2)}, u32[]{:S(2)}) collective-permute-start(bf16[160,1024]{1,0:T(8,128)(2,1)S(1)} %collective-permute-done.20.refs_12_.refs_7_), channel_id=1, source_target_pairs={{0,1},{1,0},{2,3},{3,2},{4,5},{5,4},{6,7},{7,6},{8,9},{9,8},{10,11... | collective-permute-start | bytes 983048 | tf_op jit(solution)/shard_map/ppermute | solution.py:41
  67.3 26.9 %collective-permute-start.25 = (bf16[160,1024]{1,0:T(8,128)(2,1)S(1)}, bf16[160,1024]{1,0:T(8,128)(2,1)S(1)}, u32[]{:S(2)}, u32[]{:S(2)}) collective-permute-start(bf16[160,1024]{1,0:T(8,128)(2,1)S(1)} %collective-permute-done.21.refs_13_.refs_8_), channel_id=1, source_target_pairs={{0,1},{1,0},{2,3},{3,2},{4,5},{5,4},{6,7},{7,6},{8,9},{9,8},{10,11... | collective-permute-start | bytes 983048 | tf_op jit(solution)/shard_map/ppermute | solution.py:41
  67.3 27.4 %collective-permute-start.26 = (bf16[160,1024]{1,0:T(8,128)(2,1)S(1)}, bf16[160,1024]{1,0:T(8,128)(2,1)S(1)}, u32[]{:S(2)}, u32[]{:S(2)}) collective-permute-start(bf16[160,1024]{1,0:T(8,128)(2,1)S(1)} %collective-permute-done.22.refs_14_.refs_9_), channel_id=1, source_target_pairs={{0,1},{1,0},{2,3},{3,2},{4,5},{5,4},{6,7},{7,6},{8,9},{9,8},{10,11... | collective-permute-start | bytes 983048 | tf_op jit(solution)/shard_map/ppermute | solution.py:41
  71.6 14.0 %collective-permute-start.31 = (bf16[128,384]{1,0:T(8,128)(2,1)S(1)}, bf16[128,384]{1,0:T(8,128)(2,1)S(1)}, u32[]{:S(2)}, u32[]{:S(2)}) collective-permute-start(bf16[128,384]{1,0:T(8,128)(2,1)S(1)} %get-tuple-element.29), channel_id=1, source_target_pairs={{0,2},{1,3},{2,0},{3,1},{4,6},{5,7},{6,4},{7,5},{8,10},{9,11},{10,... | collective-permute-start | bytes 294920 | tf_op jit(solution)/shard_map/ppermute | solution.py:41
  79.1 10.6 %collective-permute-start.32 = (bf16[128,384]{1,0:T(8,128)(2,1)S(1)}, bf16[128,384]{1,0:T(8,128)(2,1)S(1)}, u32[]{:S(2)}, u32[]{:S(2)}) collective-permute-start(bf16[128,384]{1,0:T(8,128)(2,1)S(1)} %get-tuple-element.30), channel_id=1, source_target_pairs={{0,4},{1,5},{2,6},{3,7},{4,0},{5,1},{6,2},{7,3},{8,12},{9,13},{10,... | collective-permute-start | bytes 294920 | tf_op jit(solution)/shard_map/ppermute | solution.py:41
  80.4 25.2 %copy-start.3 = (bf16[128,1024]{1,0:T(8,128)(2,1)S(1)}, bf16[128,1024]{1,0:T(8,128)(2,1)}, u32[]{:S(2)}) copy-start(bf16[128,1024]{1,0:T(8,128)(2,1)} %refs_7_.3) | copy-start | bytes 786436
  80.4 25.2 %copy-start.5 = (bf16[128,1024]{1,0:T(8,128)(2,1)S(1)}, bf16[128,1024]{1,0:T(8,128)(2,1)}, u32[]{:S(2)}) copy-start(bf16[128,1024]{1,0:T(8,128)(2,1)} %copy-done.4) | copy-start | bytes 786436
  80.4 25.2 %copy-start.7 = (bf16[128,1024]{1,0:T(8,128)(2,1)S(1)}, bf16[128,1024]{1,0:T(8,128)(2,1)}, u32[]{:S(2)}) copy-start(bf16[128,1024]{1,0:T(8,128)(2,1)} %copy-done.6) | copy-start | bytes 786436
  80.4 25.2 %copy-start.9 = (bf16[128,1024]{1,0:T(8,128)(2,1)S(1)}, bf16[128,1024]{1,0:T(8,128)(2,1)}, u32[]{:S(2)}) copy-start(bf16[128,1024]{1,0:T(8,128)(2,1)} %copy-done.8) | copy-start | bytes 786436
  80.5 25.2 %copy-start.23 = (f32[1024]{0:T(1024)S(1)}, f32[1024]{0:T(1024)}, u32[]{:S(2)}) copy-start(f32[1024]{0:T(1024)} %param.17) | copy-start | bytes 12292
  80.5 10.9 %collective-permute-start.33 = (bf16[128,384]{1,0:T(8,128)(2,1)S(1)}, bf16[128,384]{1,0:T(8,128)(2,1)S(1)}, u32[]{:S(2)}, u32[]{:S(2)}) collective-permute-start(bf16[128,384]{1,0:T(8,128)(2,1)S(1)} %get-tuple-element.31), channel_id=1, source_target_pairs={{0,6},{1,7},{2,4},{3,5},{4,2},{5,3},{6,0},{7,1},{8,14},{9,15},{10,... | collective-permute-start | bytes 294920 | tf_op jit(solution)/shard_map/ppermute | solution.py:41
  85.6 10.8 %collective-permute-start.17 = (bf16[512,256]{1,0:T(8,128)(2,1)S(1)}, bf16[512,256]{1,0:T(8,128)(2,1)S(1)}, u32[]{:S(2)}, u32[]{:S(2)}) collective-permute-start(bf16[512,256]{1,0:T(8,128)(2,1)S(1)} %get-tuple-element.20), channel_id=1, source_target_pairs={{0,8},{8,0},{16,24},{24,16},{1,9},{9,1},{17,25},{25,17},{2,10},{10... | collective-permute-start | bytes 786440 | tf_op jit(solution)/shard_map/ppermute | solution.py:41
  89.7 16.0 %collective-permute-start.18 = (bf16[512,256]{1,0:T(8,128)(2,1)S(1)}, bf16[512,256]{1,0:T(8,128)(2,1)S(1)}, u32[]{:S(2)}, u32[]{:S(2)}) collective-permute-start(bf16[512,256]{1,0:T(8,128)(2,1)S(1)} %get-tuple-element.21), channel_id=1, source_target_pairs={{0,16},{8,24},{16,0},{24,8},{1,17},{9,25},{17,1},{25,9},{2,18},{10... | collective-permute-start | bytes 786440 | tf_op jit(solution)/shard_map/ppermute | solution.py:41
  91.3 14.3 %collective-permute-start.19 = (bf16[512,256]{1,0:T(8,128)(2,1)S(1)}, bf16[512,256]{1,0:T(8,128)(2,1)S(1)}, u32[]{:S(2)}, u32[]{:S(2)}) collective-permute-start(bf16[512,256]{1,0:T(8,128)(2,1)S(1)} %get-tuple-element.22), channel_id=1, source_target_pairs={{0,24},{8,16},{16,8},{24,0},{1,25},{9,17},{17,9},{25,1},{2,26},{10... | collective-permute-start | bytes 786440 | tf_op jit(solution)/shard_map/ppermute | solution.py:41
  94.3 19.5 %collective-permute-start.34 = (f32[128,256]{1,0:T(8,128)S(1)}, f32[128,256]{1,0:T(8,128)S(1)}, u32[]{:S(2)}, u32[]{:S(2)}) collective-permute-start(f32[128,256]{1,0:T(8,128)S(1)} %shard_map.145.refs_1_), channel_id=1, source_target_pairs={{0,8},{8,0},{16,24},{24,16},{1,9},{9,1},{17,25},{25,17},{2,10},{10... | collective-permute-start | bytes 393224 | tf_op jit(solution)/shard_map/ppermute | solution.py:41
  94.7 21.5 %collective-permute-start.35 = (f32[128,256]{1,0:T(8,128)S(1)}, f32[128,256]{1,0:T(8,128)}, u32[]{:S(2)}, u32[]{:S(2)}) collective-permute-start(f32[128,256]{1,0:T(8,128)S(1)} %shard_map.145.refs_1_), channel_id=1, source_target_pairs={{0,16},{8,24},{16,0},{24,8},{1,17},{9,25},{17,1},{25,9},{2,18},{10... | collective-permute-start | bytes 393224 | tf_op jit(solution)/shard_map/ppermute | solution.py:41
  96.4 19.8 %collective-permute-start.36 = (f32[128,256]{1,0:T(8,128)S(1)}, f32[128,256]{1,0:T(8,128)}, u32[]{:S(2)}, u32[]{:S(2)}) collective-permute-start(f32[128,256]{1,0:T(8,128)S(1)} %shard_map.145.refs_1_), channel_id=1, source_target_pairs={{0,24},{8,16},{16,8},{24,0},{1,25},{9,17},{17,9},{25,1},{2,26},{10... | collective-permute-start | bytes 393224 | tf_op jit(solution)/shard_map/ppermute | solution.py:41
  111.2 16.7 %collective-permute-start.27 = (bf16[128,1024]{1,0:T(8,128)(2,1)}, bf16[128,1024]{1,0:T(8,128)(2,1)S(1)}, u32[]{:S(2)}, u32[]{:S(2)}) collective-permute-start(bf16[128,1024]{1,0:T(8,128)(2,1)} %get-tuple-element.25), channel_id=1, source_target_pairs={{0,8},{8,0},{16,24},{24,16},{1,9},{9,1},{17,25},{25,17},{2,10},{10... | collective-permute-start | bytes 786440 | tf_op jit(solution)/shard_map/ppermute | solution.py:41
  112.8 15.2 %collective-permute-start.28 = (bf16[128,1024]{1,0:T(8,128)(2,1)}, bf16[128,1024]{1,0:T(8,128)(2,1)}, u32[]{:S(2)}, u32[]{:S(2)}) collective-permute-start(bf16[128,1024]{1,0:T(8,128)(2,1)} %get-tuple-element.26), channel_id=1, source_target_pairs={{0,16},{8,24},{16,0},{24,8},{1,17},{9,25},{17,1},{25,9},{2,18},{10... | collective-permute-start | bytes 786440 | tf_op jit(solution)/shard_map/ppermute | solution.py:41
  113.8 0.7 copy-start.17
  114.4 13.5 %collective-permute-start.29 = (bf16[128,1024]{1,0:T(8,128)(2,1)}, bf16[128,1024]{1,0:T(8,128)(2,1)}, u32[]{:S(2)}, u32[]{:S(2)}) collective-permute-start(bf16[128,1024]{1,0:T(8,128)(2,1)} %get-tuple-element.27), channel_id=1, source_target_pairs={{0,24},{8,16},{16,8},{24,0},{1,25},{9,17},{17,9},{25,1},{2,26},{10... | collective-permute-start | bytes 786440 | tf_op jit(solution)/shard_map/ppermute | solution.py:41
  116.2 0.9 copy-start.18
  118.5 4.3 %collective-permute-start.37 = (bf16[128,256]{1,0:T(8,128)(2,1)S(1)}, bf16[128,256]{1,0:T(8,128)(2,1)S(1)}, u32[]{:S(2)}, u32[]{:S(2)}) collective-permute-start(bf16[128,256]{1,0:T(8,128)(2,1)S(1)} %shard_map.146.refs_5_), channel_id=1, source_target_pairs={{0,8},{8,0},{16,24},{24,16},{1,9},{9,1},{17,25},{25,17},{2,10},{10... | collective-permute-start | bytes 196616 | tf_op jit(solution)/shard_map/ppermute | solution.py:41
  120.1 4.7 %collective-permute-start.38 = (bf16[128,256]{1,0:T(8,128)(2,1)S(1)}, bf16[128,256]{1,0:T(8,128)(2,1)S(1)}, u32[]{:S(2)}, u32[]{:S(2)}) collective-permute-start(bf16[128,256]{1,0:T(8,128)(2,1)S(1)} %shard_map.146.refs_5_), channel_id=1, source_target_pairs={{0,16},{8,24},{16,0},{24,8},{1,17},{9,25},{17,1},{25,9},{2,18},{10... | collective-permute-start | bytes 196616 | tf_op jit(solution)/shard_map/ppermute | solution.py:41
  122.8 5.2 %collective-permute-start.39 = (bf16[128,256]{1,0:T(8,128)(2,1)S(1)}, bf16[128,256]{1,0:T(8,128)(2,1)S(1)}, u32[]{:S(2)}, u32[]{:S(2)}) collective-permute-start(bf16[128,256]{1,0:T(8,128)(2,1)S(1)} %shard_map.146.refs_5_), channel_id=1, source_target_pairs={{0,24},{8,16},{16,8},{24,0},{1,25},{9,17},{17,9},{25,1},{2,26},{10... | collective-permute-start | bytes 196616 | tf_op jit(solution)/shard_map/ppermute | solution.py:41
where the time goes:
time: 130 us
  starting transfers between devices  56.8 us (44%)
  waiting for transfers between devices  38.8 us (30%)
  Pallas kernels  25.6 us (20%)
  local copies, waits for them, and re-layouts  7.04 us (5%)
    ppermute x40, starting transfers between devices, swap(): return lax.ppermute(x, axis, [(i, i ^ offset) for i in range(size)])  56.8 us
    ppermute x40, waiting for transfers between devices, swap(): return lax.ppermute(x, axis, [(i, i ^ offset) for i in range(size)])  38.8 us
    pallas_call x8, Pallas kernels, call(): pl.pallas_call(body, out_shape=outs, in_specs=[SMEM if x.dtype == jnp.int...  18.9 us
    unnamed x48, local copies, waits for them, and re-layouts  6.19 us
    pallas_call x1, Pallas kernels, queries(): pl.pallas_call(body, out_shape=shape((near * n_own, 2 * width), BF16), gr...  4.02 us
    pallas_call x1, Pallas kernels, prepare(): pl.pallas_call(body, out_shape=[shape(o, BF16) for o in outs], grid_spec=...  2.71 us
  transfers between devices with their start and end apart: 40, of which 11 were waited for; matrix products, arithmetic and copies ran while one was open for 1% of the time, Pallas kernels for 16%

commit v1 on v0

v1 whole, which is shorter than its diff:
```python
import functools

import jax
import jax.numpy as jnp
from jax import lax
from jax.experimental import pallas as pl
from jax.experimental.pallas import tpu as pltpu
from jax.sharding import PartitionSpec as P


HEAD_DIM = 64
NORM_EPS = 1e-06
LOG2E = 1.4426950408889634
RATE = HEAD_DIM ** (-0.5) * LOG2E
LANES = 128
MLP_PEERS = 4
BF16 = jnp.bfloat16
F32 = jnp.float32
AVERAGE = BF16


VMEM = pl.BlockSpec(memory_space=pltpu.VMEM)
HBM = pl.BlockSpec(memory_space=pltpu.HBM)


def normalize(values):
    return values * lax.rsqrt(jnp.mean(values * values, axis=-1, keepdims=True) + NORM_EPS)


def project(left_side, right_side):
    return jnp.dot(left_side, right_side, preferred_element_type=F32)


def project_t(left_side, right_side):
    return lax.dot_general(
        left_side, right_side, (((1,), (1,)), ((), ())), preferred_element_type=F32
    )


def swap(x, axis, offset):
    size = lax.axis_size(axis)
    return lax.ppermute(x, axis, [(i, i ^ offset) for i in range(size)])


def gathered(x, axis, step):
    size = lax.axis_size(axis)
    return [x] + [swap(x, axis, k) for k in range(step, size, step)]


def call(body, outs, ins, flops, scratch=(), left=(), grant=48 * 1024 * 1024):
    moved = sum(x.size * x.dtype.itemsize for x in ins) + sum(
        o.size * o.dtype.itemsize for o in outs
    )
    return pl.pallas_call(
        body,
        out_shape=outs,
        in_specs=[HBM if i in left else VMEM for i in range(len(ins))],
        out_specs=[VMEM] * len(outs),
        scratch_shapes=list(scratch),
        compiler_params=pltpu.CompilerParams(vmem_limit_bytes=grant),
        cost_estimate=pl.CostEstimate(flops=flops, bytes_accessed=moved, transcendentals=0),
    )(*ins)


def aligned(index, multiple):
    return pl.multiple_of(index * multiple, multiple)


def shape(dims, dtype):
    return jax.ShapeDtypeStruct(dims, dtype)


def head_lanes(width):
    return lax.broadcasted_iota(jnp.int32, (1, width), 1) // HEAD_DIM


def only(values, lanes, head):
    return jnp.where(lanes == head, values, jnp.zeros_like(values))


def side_by_side(pair, width):
    pad = ((0, 0), (0, -width % LANES))
    return jnp.concatenate([jnp.pad(w, pad) for w in pair], 1)


def from_group(x, size, dim):
    return lax.dynamic_slice_in_dim(x, lax.axis_index("group") * size, size, dim)


def queries(tok_near, gain, w_ref, width):
    near = len(tok_near)
    n_own, features = tok_near[0].shape
    if width % LANES:
        normed = (normalize(jnp.concatenate(tok_near, 0).astype(F32)) * gain).astype(BF16)
        return project(normed, from_group(w_ref, width, 1)).astype(BF16), normed

    def body(*refs):
        gain_ref, ref_w, out, normed = refs[near:]
        for k in range(near):
            rows = slice(k * n_own, (k + 1) * n_own)
            normed[rows, :] = (normalize(refs[k][...].astype(F32)) * gain_ref[...]).astype(BF16)
        cols = pl.ds(aligned(lax.axis_index("group"), width), width)
        out[...] = project(normed[...], ref_w[:, cols]).astype(BF16)

    return call(
        body,
        [shape((near * n_own, width), BF16), shape((near * n_own, features), BF16)],
        [*tok_near, gain.reshape(1, -1), w_ref],
        2 * near * n_own * features * width,
    )


def values(normed, w_val, width):
    rows, features = normed.shape
    if width % LANES:
        return project(normed, from_group(w_val, width, 1)).astype(BF16)

    def body(normed_ref, val_w, out):
        cols = pl.ds(aligned(lax.axis_index("group"), width), width)
        out[...] = project(normed_ref[...], val_w[:, cols]).astype(BF16)

    outs = [shape((rows, width), BF16)]
    return call(body, outs, [normed, w_val], 2 * rows * features * width)[0]


def prepare(latents, gain, w_ref, w_val, w_out, w_up, w_down):
    n_group = lax.axis_size("group")
    rows, features = latents.shape
    share, width = rows // n_group, features // n_group
    ff = w_up.shape[1] // n_group
    w_rows = w_ref.shape[0]
    if width % LANES or share % 16 or ff % 16 or LANES % ff:
        lat = normalize(from_group(latents, share, 0).astype(F32)) * gain
        return (
            lat.astype(BF16),
            side_by_side([from_group(w, width, 1) for w in (w_ref, w_val)], width),
            from_group(w_out, width, 1),
            jnp.concatenate([jnp.transpose(from_group(w_up, ff, 1)), from_group(w_down, ff, 0)], 0),
        )

    def body(*refs):
        lat_in, gain_in, ref_w, val_w, out_w, up_w, down_w, lat, cols, out_cols, rest = refs[:11]
        lat_rows, up_cols, turned, sems = refs[11:]
        g = lax.axis_index("group")
        mine = pl.ds(aligned(g, width), width)
        pairs = [
            (lat_in.at[pl.ds(aligned(g, share), share), :], lat_rows),
            (up_w.at[:, pl.ds(aligned(g // (LANES // ff), LANES), LANES)], up_cols),
            (ref_w.at[:, mine], cols.at[:, :width]),
            (val_w.at[:, mine], cols.at[:, width:]),
            (out_w.at[:, mine], out_cols),
            (down_w.at[pl.ds(aligned(g, ff), ff), :], rest.at[ff:, :]),
        ]
        copies = [
            pltpu.make_async_copy(source, to, sems.at[i]) for i, (source, to) in enumerate(pairs)
        ]
        for copy in copies:
            copy.start()
        copies[0].wait()
        lat[...] = (normalize(lat_rows[...].astype(F32)) * gain_in[...]).astype(BF16)
        copies[1].wait()
        turned[...] = jnp.transpose(up_cols[...].astype(F32))
        first = aligned(lax.rem(g, LANES // ff), ff)
        rest[:ff, :] = turned[pl.ds(first, ff), :].astype(BF16)
        for copy in copies[2:]:
            copy.wait()

    outs = ((share, features), (w_rows, 2 * width), (w_rows, width), (2 * ff, features))
    return call(
        body,
        [shape(o, BF16) for o in outs],
        [latents, gain.reshape(1, -1), w_ref, w_val, w_out, w_up, w_down],
        0,
        [
            pltpu.VMEM((share, features), BF16),
            pltpu.VMEM((features, LANES), BF16),
            pltpu.VMEM((LANES, features), F32),
            pltpu.SemaphoreType.DMA((6,)),
        ],
        left=(0, 2, 3, 4, 5, 6),
        grant=None,
    )


def stack_rows(parts):
    rows, cols = parts[0].shape

    def body(*refs):
        for k, part in enumerate(refs[:-1]):
            refs[-1][k * rows : (k + 1) * rows, :] = part[...]

    return call(body, [shape((len(parts) * rows, cols), parts[0].dtype)], parts, 0)[0]


def keys(lat_near, w_own, w_far):
    near, n_z = len(lat_near), len(w_own)
    rows, features = lat_near[0].shape
    w_rows, cols = w_own[0].shape

    def body(*refs):
        lats = refs[:near]
        own, far = refs[near : near + n_z], refs[near + n_z : near + 2 * n_z]
        m = lax.axis_index("member")
        out, w_all, lat_all = refs[-3:]
        for core, pieces in enumerate((own, far)):
            for j, piece in enumerate(pieces):
                w_all[pl.ds(aligned(m ^ (2 * j + core), w_rows), w_rows), :] = piece[...]
        for k in range(near):
            lat_all[k * rows : (k + 1) * rows, :] = lats[k][...]
        out[...] = project(lat_all[...], w_all[...]).astype(BF16)

    return call(
        body,
        [shape((near * rows, cols), BF16)],
        [*lat_near, *w_own, *w_far],
        2 * near * rows * features * cols,
        [pltpu.VMEM((features, cols), BF16), pltpu.VMEM((near * rows, features), BF16)],
    )[0]


def columns(q_own, q_far, v_own, v_far, kv_own, near, n_z, share, width):
    n_tok, pad = q_own.shape[0], kv_own.shape[1] // 2
    heads = width // HEAD_DIM
    block = n_z * share
    group = 2 if near % 2 == 0 else 1
    step = group * block

    def body(own, far, own_v, far_v, k_ref, *outs):
        lanes = head_lanes(width)
        stat_lanes = lax.broadcasted_iota(jnp.int32, (1, LANES), 1)
        for first in range(0, near, group):
            k_rows = k_ref[first * block : first * block + step, :width]
            mixed = jnp.zeros((step, width), F32)
            scale = jnp.zeros((step, width), F32)
            stats = jnp.zeros((step, LANES), F32)
            for head in range(heads):
                k_head = only(k_rows, lanes, head)
                scores = [project_t(k_head, q[...]) for q in (own, far)]
                peak = jnp.maximum(*[jnp.max(s, axis=1, keepdims=True) for s in scores])
                powers = [jnp.exp2((s - peak) * RATE) for s in scores]
                total = sum(jnp.sum(e, axis=1, keepdims=True) for e in powers)
                for e, v in zip(powers, (own_v, far_v)):
                    mixed += project(e.astype(BF16), only(v[...], lanes, head))
                scale = jnp.where(lanes == head, 1.0 / total, scale)
                stats = jnp.where(stat_lanes == head, peak * RATE + jnp.log2(total), stats)
            mixed = (mixed * scale).astype(BF16)
            high = stats.astype(BF16).astype(F32)
            middle = (stats - high).astype(BF16).astype(F32)
            low = stats - high - middle
            packed = high + pltpu.roll(middle, 32, 1) + pltpu.roll(low, 64, 1)
            packed = packed.astype(BF16)
            for k in range(group):
                for j in range(n_z):
                    rows = slice(k * block + j * share, k * block + (j + 1) * share)
                    to = slice((first + k) * share, (first + k + 1) * share)
                    outs[j][to, :width] = mixed[rows]
                    if width < pad:
                        outs[j][to, width:pad] = jnp.zeros((share, pad - width), BF16)
                    outs[j][to, pad:] = packed[rows]

    outs = [shape((near * share, pad + LANES), BF16)] * n_z
    flops = 16 * near * block * n_tok * width
    return call(body, outs, [q_own, q_far, v_own, v_far, kv_own], flops)


def rows_part(q, kv_own, kv_far, n_own, peers):
    n_tok, width = q.shape
    half, pad2 = kv_own.shape
    pad = pad2 // 2
    heads = width // HEAD_DIM
    near = n_tok // n_own

    def body(q_ref, own, far, *outs):
        lanes = head_lanes(width)
        group = 2 if near % 2 == 0 else 1
        for first in range(0, near, group):
            q_rows = q_ref[first * n_own : (first + group) * n_own, :]
            mixed = jnp.zeros((group * n_own, width), F32)
            for head in range(heads):
                q_head = only(q_rows, lanes, head)
                s_own = project_t(q_head, own[:, :width])
                s_far = project_t(q_head, far[:, :width])
                peak = jnp.maximum(
                    jnp.max(s_own, axis=1, keepdims=True), jnp.max(s_far, axis=1, keepdims=True)
                )
                e_own = jnp.exp2((s_own - peak) * RATE)
                e_far = jnp.exp2((s_far - peak) * RATE)
                inverse = 1.0 / (
                    jnp.sum(e_own, axis=1, keepdims=True) + jnp.sum(e_far, axis=1, keepdims=True)
                )
                mixed += project(
                    (e_own * inverse).astype(BF16), only(own[:, pad : pad + width], lanes, head)
                )
                mixed += project(
                    (e_far * inverse).astype(BF16), only(far[:, pad : pad + width], lanes, head)
                )
            mixed = mixed.astype(BF16)
            for b in range(group):
                for k in range(near):
                    t = (first + b) ^ k
                    if t < peers:
                        outs[k][t * n_own : (t + 1) * n_own, :] = mixed[
                            b * n_own : (b + 1) * n_own
                        ]

    outs = [shape((peers * n_own, width), BF16)] * near
    return call(body, outs, [q, kv_own, kv_far], 8 * half * n_tok * width * 2)


def spread(stats, heads):
    rows = stats.shape[0]
    return jnp.concatenate(
        [jnp.broadcast_to(stats[:, h : h + 1], (rows, HEAD_DIM)) for h in range(heads)], 1
    )


def weighted(parts, stats, heads):
    peak = functools.reduce(jnp.maximum, stats)
    weights = [jnp.exp2(s - peak) for s in stats]
    total = sum(weights)
    inverse = 1.0 / total
    mixed = sum(a * spread(w * inverse, heads) for a, w in zip(parts, weights))
    return mixed


def join_members(parts, near, share, width):
    lat_own = parts[0].shape[0]
    pad = parts[0].shape[1] - LANES
    heads = width // HEAD_DIM

    def body(*refs):
        ins, out = refs[:-1], refs[-1]
        g = lax.axis_index("group")
        packed = [p[:, pad:].astype(F32) for p in ins]
        stats = [s + pltpu.roll(s, LANES - 32, 1) + pltpu.roll(s, LANES - 64, 1) for s in packed]
        mixed = weighted([p[:, :width].astype(F32) for p in ins], stats, heads)
        for k in range(near):
            first = k * share if share % 16 else aligned(g ^ k, share)
            out[pl.ds(first, share), :] = mixed[k * share : (k + 1) * share].astype(out.dtype)

    joined = call(body, [shape((lat_own, width), AVERAGE)], parts, 0)[0]
    if share % 16:
        order = jnp.arange(near) ^ lax.axis_index("group")
        blocks = jnp.take(joined.reshape(near, share, width), order, axis=0)
        joined = blocks.reshape(lat_own, width)
    return joined


def latents_part(near_avg, lat_cols, own, far):
    near, n_z = len(near_avg), len(own)
    lat_own, width = near_avg[0].shape
    w_rows = own[0].shape[0]
    features = near * width

    def body(*refs):
        avgs, lat = refs[:near], refs[near]
        own_w, far_w = refs[1 + near : 1 + near + n_z], refs[1 + near + n_z : 1 + near + 2 * n_z]
        g, m = lax.axis_index("group"), lax.axis_index("member")
        out, w_all = refs[-2:]
        for core, pieces in enumerate((own_w, far_w)):
            for j, piece in enumerate(pieces):
                to = aligned(m ^ (2 * j + core), w_rows)
                w_all[pl.ds(to, w_rows), :] = piece[...].astype(F32)
        values = [a[...].astype(F32) for a in avgs]
        square = sum(jnp.sum(a * a, axis=1, keepdims=True) for a in values)
        rate = lax.rsqrt(square * (1.0 / features) + NORM_EPS)
        if width % LANES == 0:
            total = lat[:, pl.ds(aligned(g, width), width)].astype(F32)
        else:
            total = lat[...].astype(F32)
        for k in range(near):
            total += project(
                (values[k] * rate).astype(BF16),
                w_all[pl.ds(aligned(g ^ k, width), width), :].astype(BF16),
            )
        out[...] = total.astype(BF16)

    return call(
        body,
        [shape((lat_own, width), BF16)],
        [*near_avg, lat_cols, *own, *far],
        2 * lat_own * features * width,
        [pltpu.VMEM((features, width), F32)],
    )[0]


def token_mlp(parts, tok_near, w_out, gain, own, far, n_share):
    near, peers, n_ff = len(parts), len(tok_near), len(own) + len(far)
    width = parts[0].shape[1]
    n_own, features = tok_near[0].shape

    def body(*refs):
        g = lax.axis_index("group")
        w_ref, gain_ref = refs[:2]
        ins = refs[2 : 2 + near]
        toks = refs[2 + near : 2 + near + peers]
        ff = refs[2 + near + peers : 2 + near + peers + n_ff]
        own_out, sends = refs[2 + near + peers + n_ff], refs[3 + near + peers + n_ff : -2]
        up_t, down = refs[-2:]
        for i, piece in enumerate(ff):
            rows = slice(i * n_share, (i + 1) * n_share)
            up_t[rows, :] = piece[:n_share, :]
            down[rows, :] = piece[n_share : 2 * n_share, :]
        group = 2 if peers % 2 == 0 else 1
        for t in range(0, peers, group):
            rows = slice(t * n_own, (t + group) * n_own)
            mid = jnp.concatenate([toks[t + b][...].astype(F32) for b in range(group)], 0)
            for k in range(near):
                mid += project(
                    ins[k][rows, :], w_ref[pl.ds(aligned(g ^ k, width), width), :]
                )
            mlp_in = (normalize(mid) * gain_ref[...]).astype(BF16)
            hidden = project_t(mlp_in, up_t[...])
            hidden = (hidden * (0.5 + 0.5 * lax.erf(hidden * (0.5**0.5)))).astype(BF16)
            partial = project(hidden, down[...])
            for b in range(group):
                rows = slice(b * n_own, (b + 1) * n_own)
                if t + b == 0:
                    own_out[...] = mid[rows] + partial[rows]
                else:
                    sends[t + b - 1][...] = partial[rows].astype(BF16)

    ff_rows = n_ff * n_share
    return call(
        body,
        [shape((n_own, features), F32)] + [shape((n_own, features), BF16)] * (peers - 1),
        [w_out, gain.reshape(1, -1), *parts, *tok_near, *own, *far],
        2 * peers * n_own * features * (features + 2 * ff_rows),
        [pltpu.VMEM((ff_rows, features), BF16)] * 2,
    )


def add_up(own, received):
    def body(*refs):
        refs[-1][...] = sum(r[...].astype(F32) for r in refs[:-1]).astype(BF16)

    return call(body, [shape(own.shape, BF16)], [own, *received], 0)[0]


def place_columns(parts):
    rows, width = parts[0].shape
    near = len(parts)
    if width % LANES:
        order = jnp.arange(near) ^ lax.axis_index("group")
        placed = jnp.transpose(jnp.take(jnp.stack(parts), order, axis=0), (1, 0, 2))
        return placed.reshape(rows, near * width)

    def body(*refs):
        g = lax.axis_index("group")
        for k, part in enumerate(refs[:-1]):
            refs[-1][:, pl.ds(aligned(g ^ k, width), width)] = part[...]

    outs = [shape((rows, near * width), BF16)]
    return call(body, outs, parts, 0)[0]


def per_device(
    tokens,
    latents,
    tok_gain,
    lat_gain,
    mlp_gain,
    w_ref_tok,
    w_val_tok,
    w_out_tok,
    w_ref_lat,
    w_val_lat,
    w_out_lat,
    w_up,
    w_down,
):
    n_group, n_member = lax.axis_size("group"), lax.axis_size("member")
    n_z = n_member // 2
    n_own, features = tokens.shape
    lat_own = latents.shape[0]
    width, share = features // n_group, lat_own // n_group
    ff_share = w_up.shape[1] // n_group
    peers = min(n_group, MLP_PEERS)

    tok_near = gathered(tokens, "group", 1)
    lat_part, w_mine, out_mine, ff_mine = prepare(
        latents, lat_gain, w_ref_lat, w_val_lat, w_out_lat, w_up, w_down
    )
    lat_col = gathered(lat_part, "member", 2)
    w_own = gathered(w_mine, "member", 2)
    lat_near = gathered(stack_rows(lat_col), "group", 1)
    ff_own = gathered(ff_mine, "member", 2)
    out_own = gathered(out_mine, "member", 2)
    out_far = [swap(w, "member", 1) for w in out_own]
    w_far = [swap(w, "member", 1) for w in w_own]
    ff_far = [swap(f, "member", 1) for f in ff_own]
    extra = [swap(f, "group", k) for k in range(peers, n_group, peers) for f in ff_own]
    extra_far = [swap(f, "member", 1) for f in extra]

    q, normed = queries(tok_near, tok_gain, w_ref_tok, width)
    kv_own = keys(lat_near, w_own, w_far)
    kv_far = swap(kv_own, "member", 1)
    v = values(normed, w_val_tok, width)
    q_far, v_far = swap(q, "member", 1), swap(v, "member", 1)

    row_parts = rows_part(q, kv_own, kv_far, n_own, peers)
    row_parts = [row_parts[0]] + [swap(row_parts[k], "group", k) for k in range(1, n_group)]
    pieces = columns(q, q_far, v, v_far, kv_own, n_group, n_z, share, width)
    pieces = [pieces[0]] + [swap(pieces[j], "member", 2 * j) for j in range(1, n_z)]
    own_avg = join_members(pieces, n_group, share, width)
    avg_near = gathered(own_avg, "group", 1)
    mid, *sends = token_mlp(
        row_parts,
        tok_near[:peers],
        w_out_tok,
        mlp_gain,
        ff_own + extra,
        ff_far + extra_far,
        ff_share,
    )
    received = [swap(s, "group", k + 1) for k, s in enumerate(sends)]
    lat_cols = latents if width % LANES == 0 else from_group(latents, width, 1)
    lat_new = latents_part(avg_near, lat_cols, out_own, out_far)
    lat_parts = gathered(lat_new, "group", 1)
    return add_up(mid, received), place_columns(lat_parts)


def solution(mesh):
    in_specs = (
        P(("group", "member"), None),
        P("member", None),
        P(),
        P(),
        P(),
        P(),
        P(),
        P(),
        P("member", None),
        P("member", None),
        P("member", None),
        P(None, "member"),
        P("member", None),
    )
    out_specs = (P(("group", "member"), None), P("member", None))

    return jax.shard_map(per_device, mesh=mesh, in_specs=in_specs, out_specs=out_specs, check_vma=False)
```

time: 130 us -> 146 us (1.12)
  waiting for transfers between devices: 38.8 us -> 70.3 us
  Pallas kernels: 25.6 us -> 18.7 us
  local copies, waits for them, and re-layouts: 7.04 us -> 1.78 us
  starting transfers between devices: 56.8 us -> 54.5 us
    ppermute x40 -> x48, waiting for transfers between devices: 38.8 us -> 70.3 us  [swap(): return lax.ppermute(x, axis, [(i, i ^ offset) for i in range(size)])]
    pallas_call x10 -> x12, Pallas kernels: 25.6 us -> 18.7 us  [call(): pl.pallas_call(body, out_shape=outs, in_specs=[HBM if i in left else VMEM...]
    unnamed x48 -> x20, local copies, waits for them, and re-layouts: 6.19 us -> 1.78 us
    ppermute x40 -> x48, starting transfers between devices: 56.8 us -> 54.5 us  [swap(): return lax.ppermute(x, axis, [(i, i ^ offset) for i in range(size)])]
  transfers between devices with their start and end apart: 40 -> 48, of which waited for: 11 -> 14; matrix products, arithmetic and copies ran while one was open for 1% -> 0% of each run, Pallas kernels for 16% -> 10%
where the time goes in v1:
time: 146 us
  waiting for transfers between devices  70.3 us (48%)
  starting transfers between devices  54.5 us (37%)
  Pallas kernels  18.7 us (13%)
  local copies, waits for them, and re-layouts  1.78 us (1%)
    ppermute x48, waiting for transfers between devices, swap(): return lax.ppermute(x, axis, [(i, i ^ offset) for i in range(size)])  70.3 us
    ppermute x48, starting transfers between devices, swap(): return lax.ppermute(x, axis, [(i, i ^ offset) for i in range(size)])  54.5 us
    pallas_call x12, Pallas kernels, call(): pl.pallas_call(body, out_shape=outs, in_specs=[HBM if i in left else VMEM...  18.7 us
  transfers between devices with their start and end apart: 48, of which 14 were waited for; matrix products, arithmetic and copies ran while one was open for 0% of the time, Pallas kernels for 10%

profile of v1, /device:TPU:0, one launch (start us, length us, event | category | flops | bytes accessed | tf_op | source)
XLA Modules:
  0.0 146.2 jit_solution(1621259950183273117)
XLA Ops:
  0.7 2.7 %shard_map.141 = (bf16[32,1024]{1,0:T(8,128)(2,1)}, bf16[128,512]{1,0:T(8,128)(2,1)}, bf16[128,256]{1,0:T(8,128)(2,1)}, bf16[128,1024]{1,0:T(8,128)(2,1)}) custom-call(bf16[128,1024]{1,0:T(8,128)(2,1)} %refs_4_.3, f32[1,1024]{1,0:T(1,128)} %bitcast.5, bf16[128,1024]{1,0:T(8,128)(2,1)} %refs_2_.1, bf16[128,1024]{1,0:T(8,128)(2,1)} %refs_3_.1, ...), custom_call_target="tpu_custom_call" | custom-call | bytes 2625536 | tf_op jit(solution)/shard_map/pallas_call | solution.py:54
  3.4 3.1 %collective-permute-start.9 = (bf16[128,512]{1,0:T(8,128)(2,1)}, bf16[128,512]{1,0:T(8,128)(2,1)S(1)}, u32[]{:S(2)}, u32[]{:S(2)}) collective-permute-start(bf16[128,512]{1,0:T(8,128)(2,1)} %get-tuple-element.22.refs_4_), channel_id=1, source_target_pairs={{0,2},{1,3},{2,0},{3,1},{4,6},{5,7},{6,4},{7,5},{8,10},{9,11},{10,... | collective-permute-start | bytes 393224 | tf_op jit(solution)/shard_map/ppermute | solution.py:42
  6.5 0.1 collective-permute-start.3
  6.6 3.0 %collective-permute-start.4 = (bf16[32,1024]{1,0:T(8,128)(2,1)}, bf16[32,1024]{1,0:T(8,128)(2,1)S(1)}, u32[]{:S(2)}, u32[]{:S(2)}) collective-permute-start(bf16[32,1024]{1,0:T(8,128)(2,1)} %get-tuple-element.21.refs_0_), channel_id=1, source_target_pairs={{0,4},{1,5},{2,6},{3,7},{4,0},{5,1},{6,2},{7,3},{8,12},{9,13},{10,... | collective-permute-start | bytes 196616 | tf_op jit(solution)/shard_map/ppermute | solution.py:42
  9.6 1.3 collective-permute-start.5
  10.9 1.7 %collective-permute-start.10 = (bf16[128,512]{1,0:T(8,128)(2,1)}, bf16[128,512]{1,0:T(8,128)(2,1)S(1)}, u32[]{:S(2)}, u32[]{:S(2)}) collective-permute-start(bf16[128,512]{1,0:T(8,128)(2,1)} %get-tuple-element.22.refs_4_), channel_id=1, source_target_pairs={{0,4},{1,5},{2,6},{3,7},{4,0},{5,1},{6,2},{7,3},{8,12},{9,13},{10,... | collective-permute-start | bytes 393224 | tf_op jit(solution)/shard_map/ppermute | solution.py:42
  12.6 0.4 collective-permute-done.3.refs_1_
  13.0 4.1 %collective-permute-start.11 = (bf16[128,512]{1,0:T(8,128)(2,1)}, bf16[128,512]{1,0:T(8,128)(2,1)S(1)}, u32[]{:S(2)}, u32[]{:S(2)}) collective-permute-start(bf16[128,512]{1,0:T(8,128)(2,1)} %get-tuple-element.22.refs_4_), channel_id=1, source_target_pairs={{0,6},{1,7},{2,4},{3,5},{4,2},{5,3},{6,0},{7,1},{8,14},{9,15},{10,... | collective-permute-start | bytes 393224 | tf_op jit(solution)/shard_map/ppermute | solution.py:42
  17.1 0.7 collective-permute-done.5.refs_3_
  17.9 0.8 copy-done.6
  18.7 1.6 %collective-permute-start.6 = (bf16[128,1024]{1,0:T(8,128)(2,1)S(1)}, bf16[128,1024]{1,0:T(8,128)(2,1)S(1)}, u32[]{:S(2)}, u32[]{:S(2)}) collective-permute-start(bf16[128,1024]{1,0:T(8,128)(2,1)S(1)} %shard_map.142.refs_0_), channel_id=1, source_target_pairs={{0,8},{8,0},{16,24},{24,16},{1,9},{9,1},{17,25},{25,17},{2,10},{10... | collective-permute-start | bytes 786440 | tf_op jit(solution)/shard_map/ppermute | solution.py:42
  20.3 0.5 collective-permute-start.13
  20.8 5.4 %collective-permute-done.10.refs_6_ = bf16[128,512]{1,0:T(8,128)(2,1)S(1)} collective-permute-done((bf16[128,512]{1,0:T(8,128)(2,1)}, bf16[128,512]{1,0:T(8,128)(2,1)S(1)}, u32[]{:S(2)}, u32[]{:S(2)}) %collective-permute-start.10) | collective-permute-done | bytes 131104 | tf_op jit(solution)/shard_map/ppermute | solution.py:42
  26.2 0.5 collective-permute-start.15
  26.7 1.5 %collective-permute-start.7 = (bf16[128,1024]{1,0:T(8,128)(2,1)S(1)}, bf16[128,1024]{1,0:T(8,128)(2,1)S(1)}, u32[]{:S(2)}, u32[]{:S(2)}) collective-permute-start(bf16[128,1024]{1,0:T(8,128)(2,1)S(1)} %shard_map.142.refs_0_), channel_id=1, source_target_pairs={{0,16},{8,24},{16,0},{24,8},{1,17},{9,25},{17,1},{25,9},{2,18},{10... | collective-permute-start | bytes 786440 | tf_op jit(solution)/shard_map/ppermute | solution.py:42
  28.2 1.4 collective-permute-start.8
  29.6 0.5 collective-permute-start
  30.2 1.5 %collective-permute-start.1 = (bf16[128,1024]{1,0:T(8,128)(2,1)S(1)}, bf16[128,1024]{1,0:T(8,128)(2,1)S(1)}, u32[]{:S(2)}, u32[]{:S(2)}) collective-permute-start(bf16[128,1024]{1,0:T(8,128)(2,1)S(1)} %copy-done.3), channel_id=1, source_target_pairs={{0,16},{8,24},{16,0},{24,8},{1,17},{9,25},{17,1},{25,9},{2,18},{10... | collective-permute-start | bytes 786440 | tf_op jit(solution)/shard_map/ppermute | solution.py:42
  31.7 1.4 collective-permute-start.2
  33.1 8.3 %collective-permute-done.7.refs_2_ = bf16[128,1024]{1,0:T(8,128)(2,1)S(1)} collective-permute-done((bf16[128,1024]{1,0:T(8,128)(2,1)S(1)}, bf16[128,1024]{1,0:T(8,128)(2,1)S(1)}, u32[]{:S(2)}, u32[]{:S(2)}) %collective-permute-start.7) | collective-permute-done | bytes 262176 | tf_op jit(solution)/shard_map/ppermute | solution.py:42
  41.5 1.7 %collective-permute-start.20 = (bf16[128,1024]{1,0:T(8,128)(2,1)}, bf16[128,1024]{1,0:T(8,128)(2,1)S(1)}, u32[]{:S(2)}, u32[]{:S(2)}) collective-permute-start(bf16[128,1024]{1,0:T(8,128)(2,1)} %get-tuple-element.27.refs_10_), channel_id=1, source_target_pairs={{0,2},{1,3},{2,0},{3,1},{4,6},{5,7},{6,4},{7,5},{8,10},{9,11},{10,... | collective-permute-start | bytes 786440 | tf_op jit(solution)/shard_map/ppermute | solution.py:42
  43.2 0.9 copy-done.4
  44.1 0.8 shard_map.143.own.k_ref
  45.0 0.4 collective-permute-start.38
  45.4 6.4 %collective-permute-done.1.refs_2_.refs_8_ = bf16[128,1024]{1,0:T(8,128)(2,1)S(1)} collective-permute-done((bf16[128,1024]{1,0:T(8,128)(2,1)S(1)}, bf16[128,1024]{1,0:T(8,128)(2,1)S(1)}, u32[]{:S(2)}, u32[]{:S(2)}) %collective-permute-start.1) | collective-permute-done | bytes 262176 | tf_op jit(solution)/shard_map/ppermute | solution.py:42
  51.8 0.6 shard_map.140
  52.6 0.5 shard_map.147.own_v
  53.0 0.5 collective-permute-start.31
  53.6 3.3 %collective-permute-start.39 = (bf16[128,256]{1,0:T(8,128)(2,1)S(1)}, bf16[128,256]{1,0:T(8,128)(2,1)S(1)}, u32[]{:S(2)}, u32[]{:S(2)}) collective-permute-start(bf16[128,256]{1,0:T(8,128)(2,1)S(1)} %copy-done.5), channel_id=1, source_target_pairs={{0,4},{1,5},{2,6},{3,7},{4,0},{5,1},{6,2},{7,3},{8,12},{9,13},{10,... | collective-permute-start | bytes 196616 | tf_op jit(solution)/shard_map/ppermute | solution.py:42
  56.8 3.7 %collective-permute-done.39.refs_7_ = bf16[128,256]{1,0:T(8,128)(2,1)S(1)} collective-permute-done((bf16[128,256]{1,0:T(8,128)(2,1)S(1)}, bf16[128,256]{1,0:T(8,128)(2,1)S(1)}, u32[]{:S(2)}, u32[]{:S(2)}) %collective-permute-start.39) | collective-permute-done | bytes 65568 | tf_op jit(solution)/shard_map/ppermute | solution.py:42
  60.6 0.7 collective-permute-start.40
  61.3 6.0 %collective-permute-done.40.refs_8_ = bf16[128,256]{1,0:T(8,128)(2,1)S(1)} collective-permute-done((bf16[128,256]{1,0:T(8,128)(2,1)S(1)}, bf16[128,256]{1,0:T(8,128)(2,1)S(1)}, u32[]{:S(2)}, u32[]{:S(2)}) %collective-permute-start.40) | collective-permute-done | bytes 65568 | tf_op jit(solution)/shard_map/ppermute | solution.py:42
  67.3 0.3 collective-permute-start.22
  67.5 0.5 collective-permute-start.24
  68.0 3.4 %shard_map.148 = (bf16[128,384]{1,0:T(8,128)(2,1)S(1)}, bf16[128,384]{1,0:T(8,128)(2,1)S(1)}, bf16[128,384]{1,0:T(8,128)(2,1)S(1)}, bf16[128,384]{1,0:T(8,128)(2,1)S(1)}) custom-call(bf16[512,256]{1,0:T(8,128)(2,1)S(1)} %get-tuple-element.20.q_ref.own, bf16[512,256]{1,0:T(8,128)(2,1)S(1)} %collective-permute-done.30.far, ...), custom_call_target="tpu_custom_call" | custom-call | flops 1073741824 | bytes 1966080 | tf_op jit(solution)/shard_map/pallas_call | solution.py:54
  71.4 12.2 %collective-permute-done.21.refs_12_ = bf16[128,1024]{1,0:T(8,128)(2,1)S(1)} collective-permute-done((bf16[128,1024]{1,0:T(8,128)(2,1)S(1)}, bf16[128,1024]{1,0:T(8,128)(2,1)S(1)}, u32[]{:S(2)}, u32[]{:S(2)}) %collective-permute-start.21) | collective-permute-done | bytes 262176 | tf_op jit(solution)/shard_map/ppermute | solution.py:42
  83.6 6.7 %collective-permute-start.33 = (bf16[128,384]{1,0:T(8,128)(2,1)S(1)}, bf16[128,384]{1,0:T(8,128)(2,1)S(1)}, u32[]{:S(2)}, u32[]{:S(2)}) collective-permute-start(bf16[128,384]{1,0:T(8,128)(2,1)S(1)} %get-tuple-element.35), channel_id=1, source_target_pairs={{0,4},{1,5},{2,6},{3,7},{4,0},{5,1},{6,2},{7,3},{8,12},{9,13},{10,... | collective-permute-start | bytes 294920 | tf_op jit(solution)/shard_map/ppermute | solution.py:42
  90.3 1.8 %collective-permute-start.34 = (bf16[128,384]{1,0:T(8,128)(2,1)S(1)}, bf16[128,384]{1,0:T(8,128)(2,1)S(1)}, u32[]{:S(2)}, u32[]{:S(2)}) collective-permute-start(bf16[128,384]{1,0:T(8,128)(2,1)S(1)} %get-tuple-element.36), channel_id=1, source_target_pairs={{0,6},{1,7},{2,4},{3,5},{4,2},{5,3},{6,0},{7,1},{8,14},{9,15},{10,... | collective-permute-start | bytes 294920 | tf_op jit(solution)/shard_map/ppermute | solution.py:42
  92.1 3.7 %shard_map.144 = (bf16[512,256]{1,0:T(8,128)(2,1)S(1)}, bf16[512,256]{1,0:T(8,128)(2,1)S(1)}, bf16[512,256]{1,0:T(8,128)(2,1)S(1)}, bf16[512,256]{1,0:T(8,128)(2,1)S(1)}) custom-call(bf16[512,256]{1,0:T(8,128)(2,1)S(1)} %get-tuple-element.20.q_ref.own, bf16[512,512]{1,0:T(8,128)(2,1)S(1)} %shard_map.143.own.k_ref, ...), custom_call_target="tpu_custom_call" | custom-call | flops 1073741824 | bytes 2359296 | tf_op jit(solution)/shard_map/pallas_call | solution.py:54
  95.8 0.5 collective-permute-start.26
  96.3 1.5 %collective-permute-start.17 = (bf16[512,256]{1,0:T(8,128)(2,1)S(1)}, bf16[512,256]{1,0:T(8,128)(2,1)S(1)}, u32[]{:S(2)}, u32[]{:S(2)}) collective-permute-start(bf16[512,256]{1,0:T(8,128)(2,1)S(1)} %get-tuple-element.24), channel_id=1, source_target_pairs={{0,8},{8,0},{16,24},{24,16},{1,9},{9,1},{17,25},{25,17},{2,10},{10... | collective-permute-start | bytes 786440 | tf_op jit(solution)/shard_map/ppermute | solution.py:42
  97.8 0.3 collective-permute-done.33.refs_2_
  98.1 1.5 %collective-permute-start.18 = (bf16[512,256]{1,0:T(8,128)(2,1)S(1)}, bf16[512,256]{1,0:T(8,128)(2,1)S(1)}, u32[]{:S(2)}, u32[]{:S(2)}) collective-permute-start(bf16[512,256]{1,0:T(8,128)(2,1)S(1)} %get-tuple-element.25), channel_id=1, source_target_pairs={{0,16},{8,24},{16,0},{24,8},{1,17},{9,25},{17,1},{25,9},{2,18},{10... | collective-permute-start | bytes 786440 | tf_op jit(solution)/shard_map/ppermute | solution.py:42
  99.6 1.5 collective-permute-start.19
  101.1 0.5 shard_map.149.refs_0_
  101.7 0.5 collective-permute-start.42
  102.2 3.3 %collective-permute-done.17.refs_3_ = bf16[512,256]{1,0:T(8,128)(2,1)S(1)} collective-permute-done((bf16[512,256]{1,0:T(8,128)(2,1)S(1)}, bf16[512,256]{1,0:T(8,128)(2,1)S(1)}, u32[]{:S(2)}, u32[]{:S(2)}) %collective-permute-start.17) | collective-permute-done | bytes 262176 | tf_op jit(solution)/shard_map/ppermute | solution.py:42
  105.5 6.0 %collective-permute-done.18.refs_4_ = bf16[512,256]{1,0:T(8,128)(2,1)S(1)} collective-permute-done((bf16[512,256]{1,0:T(8,128)(2,1)S(1)}, bf16[512,256]{1,0:T(8,128)(2,1)S(1)}, u32[]{:S(2)}, u32[]{:S(2)}) %collective-permute-start.18) | collective-permute-done | bytes 262176 | tf_op jit(solution)/shard_map/ppermute | solution.py:42
  111.5 1.2 collective-permute-start.35
  112.7 4.6 %shard_map.145 = (f32[128,1024]{1,0:T(8,128)S(1)}, bf16[128,1024]{1,0:T(8,128)(2,1)S(1)}, bf16[128,1024]{1,0:T(8,128)(2,1)S(1)}, bf16[128,1024]{1,0:T(8,128)(2,1)S(1)}) custom-call(bf16[1024,1024]{1,0:T(8,128)(2,1)} %refs_0_.5, f32[1,1024]{1,0:T(1,128)S(1)} %bitcast.4, bf16[512,256]{1,0:T(8,128)(2,1)S(1)} %get-tuple-element.23.refs_2_, ...), custom_call_target="tpu_custom_call" | custom-call | flops 2147483648 | bytes 7606272 | tf_op jit(solution)/shard_map/pallas_call | solution.py:54
  117.3 0.9 collective-permute-start.27
  118.1 1.5 %collective-permute-start.28 = (bf16[128,1024]{1,0:T(8,128)(2,1)S(1)}, bf16[128,1024]{1,0:T(8,128)(2,1)S(1)}, u32[]{:S(2)}, u32[]{:S(2)}) collective-permute-start(bf16[128,1024]{1,0:T(8,128)(2,1)S(1)} %get-tuple-element.30), channel_id=1, source_target_pairs={{0,16},{8,24},{16,0},{24,8},{1,17},{9,25},{17,1},{25,9},{2,18},{10... | collective-permute-start | bytes 786440 | tf_op jit(solution)/shard_map/ppermute | solution.py:42
  119.7 1.2 collective-permute-start.29
  120.8 0.8 collective-permute-start.36
  121.7 1.4 collective-permute-start.37
  123.1 11.6 %collective-permute-done.36.refs_2_ = bf16[128,256]{1,0:T(8,128)(2,1)S(1)} collective-permute-done((bf16[128,256]{1,0:T(8,128)(2,1)S(1)}, bf16[128,256]{1,0:T(8,128)(2,1)S(1)}, u32[]{:S(2)}, u32[]{:S(2)}) %collective-permute-start.36) | collective-permute-done | bytes 65568 | tf_op jit(solution)/shard_map/ppermute | solution.py:42
  134.7 0.4 shard_map.150.refs_0_
  135.1 0.4 collective-permute-start.45
  135.5 1.7 %collective-permute-start.46 = (bf16[128,256]{1,0:T(8,128)(2,1)S(1)}, bf16[128,256]{1,0:T(8,128)(2,1)S(1)}, u32[]{:S(2)}, u32[]{:S(2)}) collective-permute-start(bf16[128,256]{1,0:T(8,128)(2,1)S(1)} %shard_map.150.refs_0_), channel_id=1, source_target_pairs={{0,16},{8,24},{16,0},{24,8},{1,17},{9,25},{17,1},{25,9},{2,18},{10... | collective-permute-start | bytes 196616 | tf_op jit(solution)/shard_map/ppermute | solution.py:42
  137.2 2.2 %collective-permute-done.45.refs_1_ = bf16[128,256]{1,0:T(8,128)(2,1)S(1)} collective-permute-done((bf16[128,256]{1,0:T(8,128)(2,1)S(1)}, bf16[128,256]{1,0:T(8,128)(2,1)S(1)}, u32[]{:S(2)}, u32[]{:S(2)}) %collective-permute-start.45) | collective-permute-done | bytes 65568 | tf_op jit(solution)/shard_map/ppermute | solution.py:42
  139.4 1.5 %collective-permute-start.47 = (bf16[128,256]{1,0:T(8,128)(2,1)S(1)}, bf16[128,256]{1,0:T(8,128)(2,1)S(1)}, u32[]{:S(2)}, u32[]{:S(2)}) collective-permute-start(bf16[128,256]{1,0:T(8,128)(2,1)S(1)} %shard_map.150.refs_0_), channel_id=1, source_target_pairs={{0,24},{8,16},{16,8},{24,0},{1,25},{9,17},{17,9},{25,1},{2,26},{10... | collective-permute-start | bytes 196616 | tf_op jit(solution)/shard_map/ppermute | solution.py:42
  140.9 3.7 %collective-permute-done.47.refs_3_ = bf16[128,256]{1,0:T(8,128)(2,1)S(1)} collective-permute-done((bf16[128,256]{1,0:T(8,128)(2,1)S(1)}, bf16[128,256]{1,0:T(8,128)(2,1)S(1)}, u32[]{:S(2)}, u32[]{:S(2)}) %collective-permute-start.47) | collective-permute-done | bytes 65568 | tf_op jit(solution)/shard_map/ppermute | solution.py:42
  144.6 0.7 shard_map.151
  145.4 0.8 shard_map.146
  (64 shorter events, 0.5 us)
Async XLA Ops:
  0.6 29.0 %copy-start.3 = (bf16[128,1024]{1,0:T(8,128)(2,1)S(1)}, bf16[128,1024]{1,0:T(8,128)(2,1)}, u32[]{:S(2)}) copy-start(bf16[128,1024]{1,0:T(8,128)(2,1)} %refs_6_.3) | copy-start | bytes 786436
  0.6 51.2 %copy-start.7 = (f32[1024]{0:T(1024)S(1)}, f32[1024]{0:T(1024)}, u32[]{:S(2)}) copy-start(f32[1024]{0:T(1024)} %param.15) | copy-start | bytes 12292
  3.4 48.4 %copy-start = (bf16[1024,1024]{1,0:T(8,128)(2,1)S(1)}, bf16[1024,1024]{1,0:T(8,128)(2,1)}, u32[]{:S(2)}) copy-start(bf16[1024,1024]{1,0:T(8,128)(2,1)} %refs_5_.2) | copy-start | bytes 6291460
  3.4 16.9 %collective-permute-start.9 = (bf16[128,512]{1,0:T(8,128)(2,1)}, bf16[128,512]{1,0:T(8,128)(2,1)S(1)}, u32[]{:S(2)}, u32[]{:S(2)}) collective-permute-start(bf16[128,512]{1,0:T(8,128)(2,1)} %get-tuple-element.22.refs_4_), channel_id=1, source_target_pairs={{0,2},{1,3},{2,0},{3,1},{4,6},{5,7},{6,4},{7,5},{8,10},{9,11},{10,... | collective-permute-start | bytes 393224 | tf_op jit(solution)/shard_map/ppermute | solution.py:42
  6.5 6.5 %collective-permute-start.3 = (bf16[32,1024]{1,0:T(8,128)(2,1)}, bf16[32,1024]{1,0:T(8,128)(2,1)S(1)}, u32[]{:S(2)}, u32[]{:S(2)}) collective-permute-start(bf16[32,1024]{1,0:T(8,128)(2,1)} %get-tuple-element.21.refs_0_), channel_id=1, source_target_pairs={{0,2},{1,3},{2,0},{3,1},{4,6},{5,7},{6,4},{7,5},{8,10},{9,11},{10,... | collective-permute-start | bytes 196616 | tf_op jit(solution)/shard_map/ppermute | solution.py:42
  6.6 10.5 %collective-permute-start.4 = (bf16[32,1024]{1,0:T(8,128)(2,1)}, bf16[32,1024]{1,0:T(8,128)(2,1)S(1)}, u32[]{:S(2)}, u32[]{:S(2)}) collective-permute-start(bf16[32,1024]{1,0:T(8,128)(2,1)} %get-tuple-element.21.refs_0_), channel_id=1, source_target_pairs={{0,4},{1,5},{2,6},{3,7},{4,0},{5,1},{6,2},{7,3},{8,12},{9,13},{10,... | collective-permute-start | bytes 196616 | tf_op jit(solution)/shard_map/ppermute | solution.py:42
  9.6 8.3 %collective-permute-start.5 = (bf16[32,1024]{1,0:T(8,128)(2,1)}, bf16[32,1024]{1,0:T(8,128)(2,1)S(1)}, u32[]{:S(2)}, u32[]{:S(2)}) collective-permute-start(bf16[32,1024]{1,0:T(8,128)(2,1)} %get-tuple-element.21.refs_0_), channel_id=1, source_target_pairs={{0,6},{1,7},{2,4},{3,5},{4,2},{5,3},{6,0},{7,1},{8,14},{9,15},{10,... | collective-permute-start | bytes 196616 | tf_op jit(solution)/shard_map/ppermute | solution.py:42
  10.9 15.2 %collective-permute-start.10 = (bf16[128,512]{1,0:T(8,128)(2,1)}, bf16[128,512]{1,0:T(8,128)(2,1)S(1)}, u32[]{:S(2)}, u32[]{:S(2)}) collective-permute-start(bf16[128,512]{1,0:T(8,128)(2,1)} %get-tuple-element.22.refs_4_), channel_id=1, source_target_pairs={{0,4},{1,5},{2,6},{3,7},{4,0},{5,1},{6,2},{7,3},{8,12},{9,13},{10,... | collective-permute-start | bytes 393224 | tf_op jit(solution)/shard_map/ppermute | solution.py:42
  13.0 13.1 %collective-permute-start.11 = (bf16[128,512]{1,0:T(8,128)(2,1)}, bf16[128,512]{1,0:T(8,128)(2,1)S(1)}, u32[]{:S(2)}, u32[]{:S(2)}) collective-permute-start(bf16[128,512]{1,0:T(8,128)(2,1)} %get-tuple-element.22.refs_4_), channel_id=1, source_target_pairs={{0,6},{1,7},{2,4},{3,5},{4,2},{5,3},{6,0},{7,1},{8,14},{9,15},{10,... | collective-permute-start | bytes 393224 | tf_op jit(solution)/shard_map/ppermute | solution.py:42
  17.9 0.8 copy-start.6
  18.7 13.0 %collective-permute-start.6 = (bf16[128,1024]{1,0:T(8,128)(2,1)S(1)}, bf16[128,1024]{1,0:T(8,128)(2,1)S(1)}, u32[]{:S(2)}, u32[]{:S(2)}) collective-permute-start(bf16[128,1024]{1,0:T(8,128)(2,1)S(1)} %shard_map.142.refs_0_), channel_id=1, source_target_pairs={{0,8},{8,0},{16,24},{24,16},{1,9},{9,1},{17,25},{25,17},{2,10},{10... | collective-permute-start | bytes 786440 | tf_op jit(solution)/shard_map/ppermute | solution.py:42
  20.3 6.4 %collective-permute-start.12 = (bf16[128,512]{1,0:T(8,128)(2,1)}, bf16[128,512]{1,0:T(8,128)(2,1)S(1)}, u32[]{:S(2)}, u32[]{:S(2)}) collective-permute-start(bf16[128,512]{1,0:T(8,128)(2,1)} %get-tuple-element.22.refs_4_), channel_id=1, source_target_pairs={{0,1},{1,0},{2,3},{3,2},{4,5},{5,4},{6,7},{7,6},{8,9},{9,8},{10,11... | collective-permute-start | bytes 393224 | tf_op jit(solution)/shard_map/ppermute | solution.py:42
  20.3 7.9 %collective-permute-start.13 = (bf16[128,512]{1,0:T(8,128)(2,1)S(1)}, bf16[128,512]{1,0:T(8,128)(2,1)S(1)}, u32[]{:S(2)}, u32[]{:S(2)}) collective-permute-start(bf16[128,512]{1,0:T(8,128)(2,1)S(1)} %collective-permute-done.9.refs_5_), channel_id=1, source_target_pairs={{0,1},{1,0},{2,3},{3,2},{4,5},{5,4},{6,7},{7,6},{8,9},{9,8},{10,11... | collective-permute-start | bytes 393224 | tf_op jit(solution)/shard_map/ppermute | solution.py:42
  26.2 3.5 %collective-permute-start.14 = (bf16[128,512]{1,0:T(8,128)(2,1)S(1)}, bf16[128,512]{1,0:T(8,128)(2,1)S(1)}, u32[]{:S(2)}, u32[]{:S(2)}) collective-permute-start(bf16[128,512]{1,0:T(8,128)(2,1)S(1)} %collective-permute-done.10.refs_6_), channel_id=1, source_target_pairs={{0,1},{1,0},{2,3},{3,2},{4,5},{5,4},{6,7},{7,6},{8,9},{9,8},{10,11... | collective-permute-start | bytes 393224 | tf_op jit(solution)/shard_map/ppermute | solution.py:42
  26.2 4.0 %collective-permute-start.15 = (bf16[128,512]{1,0:T(8,128)(2,1)S(1)}, bf16[128,512]{1,0:T(8,128)(2,1)S(1)}, u32[]{:S(2)}, u32[]{:S(2)}) collective-permute-start(bf16[128,512]{1,0:T(8,128)(2,1)S(1)} %collective-permute-done.11.refs_7_), channel_id=1, source_target_pairs={{0,1},{1,0},{2,3},{3,2},{4,5},{5,4},{6,7},{7,6},{8,9},{9,8},{10,11... | collective-permute-start | bytes 393224 | tf_op jit(solution)/shard_map/ppermute | solution.py:42
  26.7 14.8 %collective-permute-start.7 = (bf16[128,1024]{1,0:T(8,128)(2,1)S(1)}, bf16[128,1024]{1,0:T(8,128)(2,1)S(1)}, u32[]{:S(2)}, u32[]{:S(2)}) collective-permute-start(bf16[128,1024]{1,0:T(8,128)(2,1)S(1)} %shard_map.142.refs_0_), channel_id=1, source_target_pairs={{0,16},{8,24},{16,0},{24,8},{1,17},{9,25},{17,1},{25,9},{2,18},{10... | collective-permute-start | bytes 786440 | tf_op jit(solution)/shard_map/ppermute | solution.py:42
  28.2 15.0 %collective-permute-start.8 = (bf16[128,1024]{1,0:T(8,128)(2,1)S(1)}, bf16[128,1024]{1,0:T(8,128)(2,1)S(1)}, u32[]{:S(2)}, u32[]{:S(2)}) collective-permute-start(bf16[128,1024]{1,0:T(8,128)(2,1)S(1)} %shard_map.142.refs_0_), channel_id=1, source_target_pairs={{0,24},{8,16},{16,8},{24,0},{1,25},{9,17},{17,9},{25,1},{2,26},{10... | collective-permute-start | bytes 786440 | tf_op jit(solution)/shard_map/ppermute | solution.py:42
  29.6 15.3 %collective-permute-start = (bf16[128,1024]{1,0:T(8,128)(2,1)S(1)}, bf16[128,1024]{1,0:T(8,128)(2,1)S(1)}, u32[]{:S(2)}, u32[]{:S(2)}) collective-permute-start(bf16[128,1024]{1,0:T(8,128)(2,1)S(1)} %copy-done.3), channel_id=1, source_target_pairs={{0,8},{8,0},{16,24},{24,16},{1,9},{9,1},{17,25},{25,17},{2,10},{10... | collective-permute-start | bytes 786440 | tf_op jit(solution)/shard_map/ppermute | solution.py:42
  30.2 21.6 %collective-permute-start.1 = (bf16[128,1024]{1,0:T(8,128)(2,1)S(1)}, bf16[128,1024]{1,0:T(8,128)(2,1)S(1)}, u32[]{:S(2)}, u32[]{:S(2)}) collective-permute-start(bf16[128,1024]{1,0:T(8,128)(2,1)S(1)} %copy-done.3), channel_id=1, source_target_pairs={{0,16},{8,24},{16,0},{24,8},{1,17},{9,25},{17,1},{25,9},{2,18},{10... | collective-permute-start | bytes 786440 | tf_op jit(solution)/shard_map/ppermute | solution.py:42
  31.7 20.1 %collective-permute-start.2 = (bf16[128,1024]{1,0:T(8,128)(2,1)S(1)}, bf16[128,1024]{1,0:T(8,128)(2,1)S(1)}, u32[]{:S(2)}, u32[]{:S(2)}) collective-permute-start(bf16[128,1024]{1,0:T(8,128)(2,1)S(1)} %copy-done.3), channel_id=1, source_target_pairs={{0,24},{8,16},{16,8},{24,0},{1,25},{9,17},{17,9},{25,1},{2,26},{10... | collective-permute-start | bytes 786440 | tf_op jit(solution)/shard_map/ppermute | solution.py:42
  41.5 25.8 %collective-permute-start.20 = (bf16[128,1024]{1,0:T(8,128)(2,1)}, bf16[128,1024]{1,0:T(8,128)(2,1)S(1)}, u32[]{:S(2)}, u32[]{:S(2)}) collective-permute-start(bf16[128,1024]{1,0:T(8,128)(2,1)} %get-tuple-element.27.refs_10_), channel_id=1, source_target_pairs={{0,2},{1,3},{2,0},{3,1},{4,6},{5,7},{6,4},{7,5},{8,10},{9,11},{10,... | collective-permute-start | bytes 786440 | tf_op jit(solution)/shard_map/ppermute | solution.py:42
  43.2 0.9 copy-start.4
  44.1 0.9 copy-start.5
  44.9 7.7 %copy-start.1 = (bf16[1024,1024]{1,0:T(8,128)(2,1)S(1)}, bf16[1024,1024]{1,0:T(8,128)(2,1)}, u32[]{:S(2)}) copy-start(bf16[1024,1024]{1,0:T(8,128)(2,1)} %val_w.1) | copy-start | bytes 6291460
  44.9 45.4 %collective-permute-start.16 = (bf16[512,512]{1,0:T(8,128)(2,1)S(1)}, bf16[512,512]{1,0:T(8,128)(2,1)S(1)}, u32[]{:S(2)}, u32[]{:S(2)}) collective-permute-start(bf16[512,512]{1,0:T(8,128)(2,1)S(1)} %shard_map.143.own.k_ref), channel_id=1, source_target_pairs={{0,1},{1,0},{2,3},{3,2},{4,5},{5,4},{6,7},{7,6},{8,9},{9,8},{10,11... | collective-permute-start | bytes 1572872 | tf_op jit(solution)/shard_map/ppermute | solution.py:42
  45.0 8.6 %collective-permute-start.38 = (bf16[128,256]{1,0:T(8,128)(2,1)S(1)}, bf16[128,256]{1,0:T(8,128)(2,1)S(1)}, u32[]{:S(2)}, u32[]{:S(2)}) collective-permute-start(bf16[128,256]{1,0:T(8,128)(2,1)S(1)} %copy-done.5), channel_id=1, source_target_pairs={{0,2},{1,3},{2,0},{3,1},{4,6},{5,7},{6,4},{7,5},{8,10},{9,11},{10,... | collective-permute-start | bytes 196616 | tf_op jit(solution)/shard_map/ppermute | solution.py:42
  52.5 14.8 %copy-start.8 = (bf16[128,1024]{1,0:T(8,128)(2,1)S(1)}, bf16[128,1024]{1,0:T(8,128)(2,1)}, u32[]{:S(2)}) copy-start(bf16[128,1024]{1,0:T(8,128)(2,1)} %get-tuple-element.27.refs_10_) | copy-start | bytes 786436
  52.5 15.1 %collective-permute-start.30 = (bf16[512,256]{1,0:T(8,128)(2,1)S(1)}, bf16[512,256]{1,0:T(8,128)(2,1)S(1)}, u32[]{:S(2)}, u32[]{:S(2)}) collective-permute-start(bf16[512,256]{1,0:T(8,128)(2,1)S(1)} %get-tuple-element.20.q_ref.own), channel_id=1, source_target_pairs={{0,1},{1,0},{2,3},{3,2},{4,5},{5,4},{6,7},{7,6},{8,9},{9,8},{10,11... | collective-permute-start | bytes 786440 | tf_op jit(solution)/shard_map/ppermute | solution.py:42
  53.0 14.5 %collective-permute-start.31 = (bf16[512,256]{1,0:T(8,128)(2,1)S(1)}, bf16[512,256]{1,0:T(8,128)(2,1)S(1)}, u32[]{:S(2)}, u32[]{:S(2)}) collective-permute-start(bf16[512,256]{1,0:T(8,128)(2,1)S(1)} %shard_map.147.own_v), channel_id=1, source_target_pairs={{0,1},{1,0},{2,3},{3,2},{4,5},{5,4},{6,7},{7,6},{8,9},{9,8},{10,11... | collective-permute-start | bytes 786440 | tf_op jit(solution)/shard_map/ppermute | solution.py:42
  53.6 7.0 %collective-permute-start.39 = (bf16[128,256]{1,0:T(8,128)(2,1)S(1)}, bf16[128,256]{1,0:T(8,128)(2,1)S(1)}, u32[]{:S(2)}, u32[]{:S(2)}) collective-permute-start(bf16[128,256]{1,0:T(8,128)(2,1)S(1)} %copy-done.5), channel_id=1, source_target_pairs={{0,4},{1,5},{2,6},{3,7},{4,0},{5,1},{6,2},{7,3},{8,12},{9,13},{10,... | collective-permute-start | bytes 196616 | tf_op jit(solution)/shard_map/ppermute | solution.py:42
  60.6 6.7 %collective-permute-start.40 = (bf16[128,256]{1,0:T(8,128)(2,1)S(1)}, bf16[128,256]{1,0:T(8,128)(2,1)S(1)}, u32[]{:S(2)}, u32[]{:S(2)}) collective-permute-start(bf16[128,256]{1,0:T(8,128)(2,1)S(1)} %copy-done.5), channel_id=1, source_target_pairs={{0,6},{1,7},{2,4},{3,5},{4,2},{5,3},{6,0},{7,1},{8,14},{9,15},{10,... | collective-permute-start | bytes 196616 | tf_op jit(solution)/shard_map/ppermute | solution.py:42
  67.2 16.4 %collective-permute-start.21 = (bf16[128,1024]{1,0:T(8,128)(2,1)S(1)}, bf16[128,1024]{1,0:T(8,128)(2,1)S(1)}, u32[]{:S(2)}, u32[]{:S(2)}) collective-permute-start(bf16[128,1024]{1,0:T(8,128)(2,1)S(1)} %copy-done.8), channel_id=1, source_target_pairs={{0,4},{1,5},{2,6},{3,7},{4,0},{5,1},{6,2},{7,3},{8,12},{9,13},{10,... | collective-permute-start | bytes 786440 | tf_op jit(solution)/shard_map/ppermute | solution.py:42
  67.3 16.3 %collective-permute-start.22 = (bf16[128,1024]{1,0:T(8,128)(2,1)S(1)}, bf16[128,1024]{1,0:T(8,128)(2,1)S(1)}, u32[]{:S(2)}, u32[]{:S(2)}) collective-permute-start(bf16[128,1024]{1,0:T(8,128)(2,1)S(1)} %copy-done.8), channel_id=1, source_target_pairs={{0,6},{1,7},{2,4},{3,5},{4,2},{5,3},{6,0},{7,1},{8,14},{9,15},{10,... | collective-permute-start | bytes 786440 | tf_op jit(solution)/shard_map/ppermute | solution.py:42
  67.5 28.2 %collective-permute-start.23 = (bf16[128,1024]{1,0:T(8,128)(2,1)S(1)}, bf16[128,1024]{1,0:T(8,128)(2,1)S(1)}, u32[]{:S(2)}, u32[]{:S(2)}) collective-permute-start(bf16[128,1024]{1,0:T(8,128)(2,1)S(1)} %copy-done.8), channel_id=1, source_target_pairs={{0,1},{1,0},{2,3},{3,2},{4,5},{5,4},{6,7},{7,6},{8,9},{9,8},{10,11... | collective-permute-start | bytes 786440 | tf_op jit(solution)/shard_map/ppermute | solution.py:42
  67.5 28.3 %collective-permute-start.24 = (bf16[128,1024]{1,0:T(8,128)(2,1)S(1)}, bf16[128,1024]{1,0:T(8,128)(2,1)S(1)}, u32[]{:S(2)}, u32[]{:S(2)}) collective-permute-start(bf16[128,1024]{1,0:T(8,128)(2,1)S(1)} %collective-permute-done.20.refs_11_), channel_id=1, source_target_pairs={{0,1},{1,0},{2,3},{3,2},{4,5},{5,4},{6,7},{7,6},{8,9},{9,8},{10,11... | collective-permute-start | bytes 786440 | tf_op jit(solution)/shard_map/ppermute | solution.py:42
  83.6 12.7 %collective-permute-start.32 = (bf16[128,384]{1,0:T(8,128)(2,1)S(1)}, bf16[128,384]{1,0:T(8,128)(2,1)S(1)}, u32[]{:S(2)}, u32[]{:S(2)}) collective-permute-start(bf16[128,384]{1,0:T(8,128)(2,1)S(1)} %get-tuple-element.34), channel_id=1, source_target_pairs={{0,2},{1,3},{2,0},{3,1},{4,6},{5,7},{6,4},{7,5},{8,10},{9,11},{10,... | collective-permute-start | bytes 294920 | tf_op jit(solution)/shard_map/ppermute | solution.py:42
  83.6 14.5 %collective-permute-start.33 = (bf16[128,384]{1,0:T(8,128)(2,1)S(1)}, bf16[128,384]{1,0:T(8,128)(2,1)S(1)}, u32[]{:S(2)}, u32[]{:S(2)}) collective-permute-start(bf16[128,384]{1,0:T(8,128)(2,1)S(1)} %get-tuple-element.35), channel_id=1, source_target_pairs={{0,4},{1,5},{2,6},{3,7},{4,0},{5,1},{6,2},{7,3},{8,12},{9,13},{10,... | collective-permute-start | bytes 294920 | tf_op jit(solution)/shard_map/ppermute | solution.py:42
  90.3 22.4 %copy-start.9 = (f32[1024]{0:T(1024)S(1)}, f32[1024]{0:T(1024)}, u32[]{:S(2)}) copy-start(f32[1024]{0:T(1024)} %param.17) | copy-start | bytes 12292
  90.3 9.4 %collective-permute-start.34 = (bf16[128,384]{1,0:T(8,128)(2,1)S(1)}, bf16[128,384]{1,0:T(8,128)(2,1)S(1)}, u32[]{:S(2)}, u32[]{:S(2)}) collective-permute-start(bf16[128,384]{1,0:T(8,128)(2,1)S(1)} %get-tuple-element.36), channel_id=1, source_target_pairs={{0,6},{1,7},{2,4},{3,5},{4,2},{5,3},{6,0},{7,1},{8,14},{9,15},{10,... | collective-permute-start | bytes 294920 | tf_op jit(solution)/shard_map/ppermute | solution.py:42
  95.7 5.9 %collective-permute-start.25 = (bf16[128,1024]{1,0:T(8,128)(2,1)S(1)}, bf16[128,1024]{1,0:T(8,128)(2,1)S(1)}, u32[]{:S(2)}, u32[]{:S(2)}) collective-permute-start(bf16[128,1024]{1,0:T(8,128)(2,1)S(1)} %collective-permute-done.21.refs_12_), channel_id=1, source_target_pairs={{0,1},{1,0},{2,3},{3,2},{4,5},{5,4},{6,7},{7,6},{8,9},{9,8},{10,11... | collective-permute-start | bytes 786440 | tf_op jit(solution)/shard_map/ppermute | solution.py:42
  95.8 5.9 %collective-permute-start.26 = (bf16[128,1024]{1,0:T(8,128)(2,1)S(1)}, bf16[128,1024]{1,0:T(8,128)(2,1)S(1)}, u32[]{:S(2)}, u32[]{:S(2)}) collective-permute-start(bf16[128,1024]{1,0:T(8,128)(2,1)S(1)} %collective-permute-done.22.refs_13_), channel_id=1, source_target_pairs={{0,1},{1,0},{2,3},{3,2},{4,5},{5,4},{6,7},{7,6},{8,9},{9,8},{10,11... | collective-permute-start | bytes 786440 | tf_op jit(solution)/shard_map/ppermute | solution.py:42
  96.3 9.2 %collective-permute-start.17 = (bf16[512,256]{1,0:T(8,128)(2,1)S(1)}, bf16[512,256]{1,0:T(8,128)(2,1)S(1)}, u32[]{:S(2)}, u32[]{:S(2)}) collective-permute-start(bf16[512,256]{1,0:T(8,128)(2,1)S(1)} %get-tuple-element.24), channel_id=1, source_target_pairs={{0,8},{8,0},{16,24},{24,16},{1,9},{9,1},{17,25},{25,17},{2,10},{10... | collective-permute-start | bytes 786440 | tf_op jit(solution)/shard_map/ppermute | solution.py:42
  98.1 13.3 %collective-permute-start.18 = (bf16[512,256]{1,0:T(8,128)(2,1)S(1)}, bf16[512,256]{1,0:T(8,128)(2,1)S(1)}, u32[]{:S(2)}, u32[]{:S(2)}) collective-permute-start(bf16[512,256]{1,0:T(8,128)(2,1)S(1)} %get-tuple-element.25), channel_id=1, source_target_pairs={{0,16},{8,24},{16,0},{24,8},{1,17},{9,25},{17,1},{25,9},{2,18},{10... | collective-permute-start | bytes 786440 | tf_op jit(solution)/shard_map/ppermute | solution.py:42
  99.6 11.8 %collective-permute-start.19 = (bf16[512,256]{1,0:T(8,128)(2,1)S(1)}, bf16[512,256]{1,0:T(8,128)(2,1)S(1)}, u32[]{:S(2)}, u32[]{:S(2)}) collective-permute-start(bf16[512,256]{1,0:T(8,128)(2,1)S(1)} %get-tuple-element.26), channel_id=1, source_target_pairs={{0,24},{8,16},{16,8},{24,0},{1,25},{9,17},{17,9},{25,1},{2,26},{10... | collective-permute-start | bytes 786440 | tf_op jit(solution)/shard_map/ppermute | solution.py:42
  101.7 15.6 %collective-permute-start.41 = (bf16[128,256]{1,0:T(8,128)(2,1)S(1)}, bf16[128,256]{1,0:T(8,128)(2,1)S(1)}, u32[]{:S(2)}, u32[]{:S(2)}) collective-permute-start(bf16[128,256]{1,0:T(8,128)(2,1)S(1)} %copy-done.5), channel_id=1, source_target_pairs={{0,1},{1,0},{2,3},{3,2},{4,5},{5,4},{6,7},{7,6},{8,9},{9,8},{10,11... | collective-permute-start | bytes 196616 | tf_op jit(solution)/shard_map/ppermute | solution.py:42
  101.7 16.4 %collective-permute-start.42 = (bf16[128,256]{1,0:T(8,128)(2,1)S(1)}, bf16[128,256]{1,0:T(8,128)(2,1)S(1)}, u32[]{:S(2)}, u32[]{:S(2)}) collective-permute-start(bf16[128,256]{1,0:T(8,128)(2,1)S(1)} %collective-permute-done.38.refs_6_), channel_id=1, source_target_pairs={{0,1},{1,0},{2,3},{3,2},{4,5},{5,4},{6,7},{7,6},{8,9},{9,8},{10,11... | collective-permute-start | bytes 196616 | tf_op jit(solution)/shard_map/ppermute | solution.py:42
  105.5 14.2 %collective-permute-start.43 = (bf16[128,256]{1,0:T(8,128)(2,1)S(1)}, bf16[128,256]{1,0:T(8,128)(2,1)S(1)}, u32[]{:S(2)}, u32[]{:S(2)}) collective-permute-start(bf16[128,256]{1,0:T(8,128)(2,1)S(1)} %collective-permute-done.39.refs_7_), channel_id=1, source_target_pairs={{0,1},{1,0},{2,3},{3,2},{4,5},{5,4},{6,7},{7,6},{8,9},{9,8},{10,11... | collective-permute-start | bytes 196616 | tf_op jit(solution)/shard_map/ppermute | solution.py:42
  111.5 9.4 %collective-permute-start.44 = (bf16[128,256]{1,0:T(8,128)(2,1)S(1)}, bf16[128,256]{1,0:T(8,128)(2,1)S(1)}, u32[]{:S(2)}, u32[]{:S(2)}) collective-permute-start(bf16[128,256]{1,0:T(8,128)(2,1)S(1)} %collective-permute-done.40.refs_8_), channel_id=1, source_target_pairs={{0,1},{1,0},{2,3},{3,2},{4,5},{5,4},{6,7},{7,6},{8,9},{9,8},{10,11... | collective-permute-start | bytes 196616 | tf_op jit(solution)/shard_map/ppermute | solution.py:42
  111.5 10.2 %collective-permute-start.35 = (bf16[128,256]{1,0:T(8,128)(2,1)S(1)}, bf16[128,256]{1,0:T(8,128)(2,1)S(1)}, u32[]{:S(2)}, u32[]{:S(2)}) collective-permute-start(bf16[128,256]{1,0:T(8,128)(2,1)S(1)} %shard_map.149.refs_0_), channel_id=1, source_target_pairs={{0,8},{8,0},{16,24},{24,16},{1,9},{9,1},{17,25},{25,17},{2,10},{10... | collective-permute-start | bytes 196616 | tf_op jit(solution)/shard_map/ppermute | solution.py:42
  112.7 22.1 %copy-start.2 = (bf16[128,1024]{1,0:T(8,128)(2,1)S(1)}, bf16[128,1024]{1,0:T(8,128)(2,1)}, u32[]{:S(2)}) copy-start(bf16[128,1024]{1,0:T(8,128)(2,1)} %refs_4_.3) | copy-start | bytes 786436
  117.3 28.1 %collective-permute-start.27 = (bf16[128,1024]{1,0:T(8,128)(2,1)S(1)}, bf16[128,1024]{1,0:T(8,128)(2,1)S(1)}, u32[]{:S(2)}, u32[]{:S(2)}) collective-permute-start(bf16[128,1024]{1,0:T(8,128)(2,1)S(1)} %get-tuple-element.29), channel_id=1, source_target_pairs={{0,8},{8,0},{16,24},{24,16},{1,9},{9,1},{17,25},{25,17},{2,10},{10... | collective-permute-start | bytes 786440 | tf_op jit(solution)/shard_map/ppermute | solution.py:42
  118.1 27.2 %collective-permute-start.28 = (bf16[128,1024]{1,0:T(8,128)(2,1)S(1)}, bf16[128,1024]{1,0:T(8,128)(2,1)S(1)}, u32[]{:S(2)}, u32[]{:S(2)}) collective-permute-start(bf16[128,1024]{1,0:T(8,128)(2,1)S(1)} %get-tuple-element.30), channel_id=1, source_target_pairs={{0,16},{8,24},{16,0},{24,8},{1,17},{9,25},{17,1},{25,9},{2,18},{10... | collective-permute-start | bytes 786440 | tf_op jit(solution)/shard_map/ppermute | solution.py:42
  119.7 25.7 %collective-permute-start.29 = (bf16[128,1024]{1,0:T(8,128)(2,1)S(1)}, bf16[128,1024]{1,0:T(8,128)(2,1)S(1)}, u32[]{:S(2)}, u32[]{:S(2)}) collective-permute-start(bf16[128,1024]{1,0:T(8,128)(2,1)S(1)} %get-tuple-element.31), channel_id=1, source_target_pairs={{0,24},{8,16},{16,8},{24,0},{1,25},{9,17},{17,9},{25,1},{2,26},{10... | collective-permute-start | bytes 786440 | tf_op jit(solution)/shard_map/ppermute | solution.py:42
  120.8 13.9 %collective-permute-start.36 = (bf16[128,256]{1,0:T(8,128)(2,1)S(1)}, bf16[128,256]{1,0:T(8,128)(2,1)S(1)}, u32[]{:S(2)}, u32[]{:S(2)}) collective-permute-start(bf16[128,256]{1,0:T(8,128)(2,1)S(1)} %shard_map.149.refs_0_), channel_id=1, source_target_pairs={{0,16},{8,24},{16,0},{24,8},{1,17},{9,25},{17,1},{25,9},{2,18},{10... | collective-permute-start | bytes 196616 | tf_op jit(solution)/shard_map/ppermute | solution.py:42
  121.7 13.1 %collective-permute-start.37 = (bf16[128,256]{1,0:T(8,128)(2,1)S(1)}, bf16[128,256]{1,0:T(8,128)(2,1)S(1)}, u32[]{:S(2)}, u32[]{:S(2)}) collective-permute-start(bf16[128,256]{1,0:T(8,128)(2,1)S(1)} %shard_map.149.refs_0_), channel_id=1, source_target_pairs={{0,24},{8,16},{16,8},{24,0},{1,25},{9,17},{17,9},{25,1},{2,26},{10... | collective-permute-start | bytes 196616 | tf_op jit(solution)/shard_map/ppermute | solution.py:42
  135.1 4.3 %collective-permute-start.45 = (bf16[128,256]{1,0:T(8,128)(2,1)S(1)}, bf16[128,256]{1,0:T(8,128)(2,1)S(1)}, u32[]{:S(2)}, u32[]{:S(2)}) collective-permute-start(bf16[128,256]{1,0:T(8,128)(2,1)S(1)} %shard_map.150.refs_0_), channel_id=1, source_target_pairs={{0,8},{8,0},{16,24},{24,16},{1,9},{9,1},{17,25},{25,17},{2,10},{10... | collective-permute-start | bytes 196616 | tf_op jit(solution)/shard_map/ppermute | solution.py:42
  135.5 5.4 %collective-permute-start.46 = (bf16[128,256]{1,0:T(8,128)(2,1)S(1)}, bf16[128,256]{1,0:T(8,128)(2,1)S(1)}, u32[]{:S(2)}, u32[]{:S(2)}) collective-permute-start(bf16[128,256]{1,0:T(8,128)(2,1)S(1)} %shard_map.150.refs_0_), channel_id=1, source_target_pairs={{0,16},{8,24},{16,0},{24,8},{1,17},{9,25},{17,1},{25,9},{2,18},{10... | collective-permute-start | bytes 196616 | tf_op jit(solution)/shard_map/ppermute | solution.py:42
  139.4 5.2 %collective-permute-start.47 = (bf16[128,256]{1,0:T(8,128)(2,1)S(1)}, bf16[128,256]{1,0:T(8,128)(2,1)S(1)}, u32[]{:S(2)}, u32[]{:S(2)}) collective-permute-start(bf16[128,256]{1,0:T(8,128)(2,1)S(1)} %shard_map.150.refs_0_), channel_id=1, source_target_pairs={{0,24},{8,16},{16,8},{24,0},{1,25},{9,17},{17,9},{25,1},{2,26},{10... | collective-permute-start | bytes 196616 | tf_op jit(solution)/shard_map/ppermute | solution.py:42
